TPU v7x, 512 devices: a whole 4x4x16 slice. The times are simulated.
512 devices in a mesh: replica: 64 (over z, y_hi, core), shard: 8 (over x, y_lo).
Axes of the slice: x: 4, y: 4 (y_hi: 2, y_lo: 2; y = y_hi * 2 + y_lo), z: 16, core: 2. Of those that a mesh axis runs over, the one named last changes fastest.
Arguments:
- frames_in: bfloat16 [512, 512, 768], P(('replica', 'shard')), may hold values from -6 to 6
- lengths: int32 [512], P(('replica', 'shard')), may hold values from 128 to 512, as said below
- up_weight: bfloat16 [768, 1536], P('shard'), may hold values from -0.21875 to 0.21875
- norm_gain: bfloat16 [768], P('shard'), may hold values from 0.25 to 1.75
- conv_kernel: bfloat16 [32, 768], P(None, 'shard'), may hold values from -1 to 1
- down_weight: bfloat16 [768, 768], P(None, 'shard'), may hold values from -0.21875 to 0.21875
- cotangent: bfloat16 [512, 512, 768], P(('replica', 'shard')), may hold values from -24 to 24
Outputs:
- result: bfloat16 [512, 512, 768], P(('replica', 'shard'))
- grad_in: bfloat16 [512, 512, 768], P(('replica', 'shard'))
- up_grad: float32 [768, 1536], P('shard')
- gain_grad: float32 [768], P('shard')
- kernel_grad: float32 [32, 768], P(None, 'shard')
- down_grad: float32 [768, 768], P(None, 'shard')
Inputs may be any that keep to these rules, and one draw needn't show every extreme that they name: `lengths`: each length is a multiple of 128; utterance 0 has 512 frames.
All inputs are finite; a program needn't handle non-finite values.
Results may differ from a plain program's by a relative error of at most 0.017.
Values may be sent and summed in bfloat16 or wider, within the bound.
A program may use at most 64 MiB of HBM per device.

v0:
```python
import jax
import jax.numpy as jnp
from jax import lax
from jax.sharding import PartitionSpec as P

EPS = 1e-05


def normalize(inputs):
    average = jnp.mean(inputs, axis=1, keepdims=True)
    centred = inputs - average
    inv_std = lax.rsqrt(jnp.mean(centred * centred, axis=1, keepdims=True) + EPS)
    return (centred * inv_std, inv_std)


def depthwise(signal, taps_f, front, back):
    frames = signal.shape[1]
    padded = jnp.pad(signal, ((0, 0), (front, back), (0, 0)))
    total = jnp.zeros_like(signal)
    for offset in range(taps_f.shape[0]):
        total = total + taps_f[offset] * padded[:, offset : offset + frames]
    return total


def tap_grads(grad, signal, front, back):
    frames = signal.shape[1]
    padded = jnp.pad(signal, ((0, 0), (front, back), (0, 0)))
    return jnp.stack(
        [
            jnp.sum(grad * padded[:, offset : offset + frames], axis=(0, 1))
            for offset in range(front + back + 1)
        ]
    )


def body(frames_in, lengths, up_weight, norm_gain, conv_kernel, down_weight, cotangent):
    utts, frames, width = frames_in.shape
    chans = up_weight.shape[1] // 2
    count_taps = conv_kernel.shape[0]
    front = count_taps // 2
    back = count_taps - 1 - front
    row_count = utts * frames
    live = (jnp.arange(frames, dtype=jnp.int32)[None, :] < lengths[:, None]).astype(jnp.float32)
    live_col = live.reshape(row_count, 1)
    inputs = frames_in.reshape(row_count, width).astype(jnp.float32)
    normed, inv_std = normalize(inputs)
    up_full, gain_bf, taps_bf = (
        lax.all_gather(up_weight, "shard", axis=0, tiled=True),
        lax.all_gather(norm_gain, "shard", axis=0, tiled=True),
        lax.all_gather(conv_kernel, "shard", axis=1, tiled=True),
    )
    gain_f = gain_bf.astype(jnp.float32)
    scaled = (normed * gain_f).astype(jnp.bfloat16)
    projected = jnp.dot(scaled, up_full, preferred_element_type=jnp.float32)
    values_half = projected[:, :chans]
    gate_sig = jax.nn.sigmoid(projected[:, chans:])
    gated = (values_half * gate_sig * live_col).astype(jnp.bfloat16)
    taps_f = taps_bf.astype(jnp.float32)
    gated_f = gated.astype(jnp.float32).reshape(utts, frames, chans)
    filtered = depthwise(gated_f, taps_f, front, back).reshape(row_count, chans)
    activated = (jax.nn.silu(filtered) * live_col).astype(jnp.bfloat16)
    upstream = cotangent.reshape(row_count, width)
    down_full = lax.all_gather(down_weight, "shard", axis=1, tiled=True)
    mixed = jnp.dot(activated, down_full, preferred_element_type=jnp.float32)
    d_act = lax.dot_general(
        upstream, down_full, (((1,), (1,)), ((), ())), preferred_element_type=jnp.float32
    )
    result = (inputs + mixed).astype(jnp.bfloat16)
    down_part = lax.dot_general(
        activated, upstream, (((0,), (0,)), ((), ())), preferred_element_type=jnp.float32
    )
    factor = 1.0 / float(utts * lax.axis_size("replica") * lax.axis_size("shard") * frames) ** 0.5
    filt_sig = jax.nn.sigmoid(filtered)
    d_filt = d_act * live_col * filt_sig * (1.0 + filtered * (1.0 - filt_sig))
    d_filt3 = d_filt.reshape(utts, frames, chans)
    kernel_part = tap_grads(d_filt3, gated_f, front, back)
    d_gated = depthwise(d_filt3, taps_f[::-1], back, front).reshape(row_count, chans) * live_col
    d_proj = jnp.concatenate(
        [d_gated * gate_sig, d_gated * values_half * gate_sig * (1.0 - gate_sig)], axis=1
    ).astype(jnp.bfloat16)
    up_part = lax.dot_general(
        scaled, d_proj, (((0,), (0,)), ((), ())), preferred_element_type=jnp.float32
    )
    d_scaled = lax.dot_general(
        d_proj, up_full, (((1,), (1,)), ((), ())), preferred_element_type=jnp.float32
    )
    gain_part = jnp.sum(d_scaled * normed, axis=0)
    d_normed = d_scaled * gain_f
    d_inputs = inv_std * (
        d_normed
        - jnp.mean(d_normed, axis=1, keepdims=True)
        - normed * jnp.mean(d_normed * normed, axis=1, keepdims=True)
    )
    grad_in = (upstream.astype(jnp.float32) + d_inputs).astype(jnp.bfloat16)
    slices = (
        lax.psum_scatter(
            up_part.astype(jnp.bfloat16), "shard", scatter_dimension=0, tiled=True
        ).astype(jnp.float32),
        lax.psum_scatter(
            gain_part.astype(jnp.bfloat16), "shard", scatter_dimension=0, tiled=True
        ).astype(jnp.float32),
        lax.psum_scatter(
            kernel_part.astype(jnp.bfloat16), "shard", scatter_dimension=1, tiled=True
        ).astype(jnp.float32),
        lax.psum_scatter(
            down_part.astype(jnp.bfloat16), "shard", scatter_dimension=1, tiled=True
        ).astype(jnp.float32),
    )
    up_total, gain_total, kernel_total, down_total = lax.psum(
        (slices[0], slices[1], slices[2], slices[3]), "replica"
    )
    return (
        result.reshape(utts, frames, width),
        grad_in.reshape(utts, frames, width),
        up_total * factor,
        gain_total * factor,
        kernel_total * factor,
        down_total * factor,
    )


def solution(mesh):
    return jax.shard_map(
        body,
        mesh=mesh,
        in_specs=(
            P(("replica", "shard"), None, None),
            P(("replica", "shard")),
            P("shard", None),
            P("shard"),
            P(None, "shard"),
            P(None, "shard"),
            P(("replica", "shard"), None, None),
        ),
        out_specs=(
            P(("replica", "shard"), None, None),
            P(("replica", "shard"), None, None),
            P("shard", None),
            P("shard"),
            P(None, "shard"),
            P(None, "shard"),
        ),
        check_vma=False,
    )
```

profile of v0, /device:TPU:1, one launch (start us, length us, event | category | flops | bytes accessed | tf_op | source)
XLA Modules:
  0.0 575.7 jit_solution(7954746644922215602)
XLA Ops:
  8.7 22.9 %all-gather = bf16[8,96,32]{1,2,0:T(8,128)(2,1)S(1)} all-gather(bf16[1,96,32]{1,2,0:T(8,128)(2,1)} %bitcast.209), channel_id=1, replica_groups=mesh['replica'=64,'shard'=8] {'shard'}, dimensions={0}, use_global_device_ids=true | all-gather | bytes 55296 | tf_op jit(solution)/shard_map/all_gather | solution.py:50
  34.8 17.1 %all-reduce.2 = bf16[768]{0:T(1024)(128)(2,1)S(1)} all-reduce(bf16[768]{0:T(1024)(128)(2,1)S(1)} %dynamic-update-slice), channel_id=1, replica_groups=mesh['replica'=64,'shard'=8] {'shard'}, use_global_device_ids=true, to_apply=%add.2 | all-reduce | flops 768 | bytes 3072
  51.9 27.2 %all-gather.4.cloned.1.call-done = bf16[768,1536]{1,0:T(8,128)(2,1)} async-done(((bf16[96,1536]{1,0:T(8,128)(2,1)}), bf16[768,1536]{1,0:T(8,128)(2,1)}) %all-gather.4.cloned.1.call-update) | async-done | bytes 2359312 | tf_op jit(solution)/shard_map/all_gather | solution.py:48
  79.1 3.1 fusion.77
  82.7 1.2 copy-done
  83.9 0.9 copy-done.4
  84.7 7.4 %fusion.33 = f32[1,512,768]{2,1,0:T(8,128)} fusion(bf16[512,768]{1,0:T(8,128)(2,1)S(1)} %get-tuple-element.79, f32[768]{0:T(1024)S(1)} %get-tuple-element.41, f32[768]{0:T(1024)S(1)} %get-tuple-element.42, f32[768]{0:T(1024)S(1)} %get-tuple-element.43, f32[768]{0:T(1024)S(1)} %get-tuple-element.44, f32[768]{0:T(1024)S(1)} %get-tuple-element.45, ...), kind=kLoop, calls=%fused_computation.39 | loop fusion | flops 25165824 | bytes 4030464 | tf_op jit(solution)/shard_map/add | solution.py:21
  92.1 33.9 %all-gather.6.cloned.1.call-done = bf16[768,768]{0,1:T(8,128)(2,1)} async-done(((bf16[768,96]{0,1:T(8,128)(2,1)}), bf16[768,768]{0,1:T(8,128)(2,1)}) %all-gather.6.cloned.1.call-update) | async-done | bytes 1179664 | tf_op jit(solution)/shard_map/all_gather | solution.py:63
  126.0 5.7 multiply_reduce_fusion.1
  131.7 4.1 multiply_reduce_fusion
  136.7 0.8 copy.15
  137.6 3.2 convolution_convert_fusion.1
  141.1 9.2 %multiply_convert_fusion.2 = (bf16[512,768]{1,0:T(8,128)(2,1)S(1)}, f32[512,768]{1,0:T(8,128)S(1)}) fusion(f32[512,1536]{1,0:T(8,128)} %copy-done, f32[512]{0:T(512)S(1)} %fusion.71, f32[768]{0:T(1024)S(1)} %get-tuple-element.40, f32[768]{0:T(1024)S(1)} %get-tuple-element.59, f32[768]{0:T(1024)S(1)} %get-tuple-element.71, f32[768]{0:T(1024)S(1)} %get-tuple-element.70, ...), kind=kLoop, calls=%fused_computation.107 | loop fusion | flops 27131904 | bytes 7178240 | tf_op jit(solution)/shard_map/convert.64
  151.8 3.0 convolution_convert_fusion
  155.5 3.9 fusion.14
  159.4 14.4 %all-reduce.3 = bf16[768]{0:T(1024)(128)(2,1)S(1)} all-reduce(bf16[768]{0:T(1024)(128)(2,1)S(1)} %get-tuple-element.37), channel_id=3, replica_groups=mesh['replica'=64,'shard'=8] {'shard'}, use_global_device_ids=true, to_apply=%region_7.8.clone | all-reduce | flops 768 | bytes 3072
  173.8 1.5 fusion.64
  175.9 1.9 fusion.62
  177.8 2.8 reduce-scatter.10.cloned.1.call-done
  180.6 0.8 copy.16
  181.4 49.1 %reduce-scatter.8.cloned.1.call-done = bf16[768,96]{0,1:T(8,128)(2,1)} async-done(((bf16[768,768]{0,1:T(8,128)(2,1)}), bf16[768,96]{0,1:T(8,128)(2,1)}) %reduce-scatter.8.cloned.1.call-update) | async-done | bytes 147472 | tf_op jit(solution)/shard_map/reduce_scatter | solution.py:105
  230.6 69.9 %reduce-scatter.6.cloned.1.call-done = bf16[96,1536]{1,0:T(8,128)(2,1)} async-done(((bf16[768,1536]{1,0:T(8,128)(2,1)}), bf16[96,1536]{1,0:T(8,128)(2,1)}) %reduce-scatter.6.cloned.1.call-update) | async-done | bytes 294928 | tf_op jit(solution)/shard_map/reduce_scatter | solution.py:96
  300.4 266.0 %all-reduce.6 = (f32[96,1536]{1,0:T(8,128)S(1)}, f32[96]{0:T(128)S(1)}, f32[32,96]{1,0:T(8,128)S(1)}, f32[768,96]{0,1:T(8,128)S(1)}) all-reduce(bf16[96,1536]{1,0:T(8,128)(2,1)} %reduce-scatter.6.cloned.1.call-done, f32[96]{0:T(128)S(1)} %dynamic-slice_convert_fusion, ...), channel_id=1, replica_groups=mesh['replica'=64,'shard'=8] {'replica'}, use_global_device_ids=true, to_apply=%region_5.6 | all-reduce | flops 224352 | bytes 1346304 | tf_op jit(solution)/shard_map/psum | solution.py:109
  566.4 0.9 broadcast_multiply_fusion
  (90 shorter events, 8.6 us)
Async XLA Ops:
  7.2 26.1 %copy-start.11 = (u32[512]{0:T(512)S(1)}, u32[512]{0:T(512)}, u32[]{:S(2)}) copy-start(u32[512]{0:T(512)} %constant.30) | copy-start | bytes 6148
  7.2 24.9 %copy-start.2 = (bf16[1,512,768]{2,1,0:T(8,128)(2,1)S(1)}, bf16[1,512,768]{2,1,0:T(8,128)(2,1)}, u32[]{:S(2)}) copy-start(bf16[1,512,768]{2,1,0:T(8,128)(2,1)} %param.7) | copy-start | bytes 2359300
  7.2 27.4 %copy-start.13 = (bf16[96]{0:T(256)(128)(2,1)S(1)}, bf16[96]{0:T(256)(128)(2,1)}, u32[]{:S(2)}) copy-start(bf16[96]{0:T(256)(128)(2,1)} %param.10) | copy-start | bytes 580
  7.2 71.9 %all-gather.4.cloned.1.call-start = ((), (), s32[]{:S(2)}) async-start(), calls=%async_computation.3 | async-start | bytes 2654208 | tf_op jit(solution)/shard_map/all_gather | solution.py:48
  7.9 118.1 %all-gather.6.cloned.1.call-start = ((), (), s32[]{:S(2)}) async-start(), calls=%async_computation.4 | async-start | bytes 1327104 | tf_op jit(solution)/shard_map/all_gather | solution.py:63
  8.7 171.9 %reduce-scatter.10.cloned.1.call-start = ((), (), s32[]{:S(2)}) async-start(), calls=%async_computation.7 | async-start | bytes 221184
  82.2 1.7 copy-start
  83.9 0.9 copy-start.4
  131.7 4.1 copy-start.5
  135.8 1.8 copy-start.6
  137.6 93.0 %reduce-scatter.8.cloned.1.call-start = ((), (), s32[]{:S(2)}) async-start(), calls=%async_computation.6 | async-start | bytes 1327104 | tf_op jit(solution)/shard_map/reduce_scatter | solution.py:105
  140.9 159.6 %reduce-scatter.6.cloned.1.call-start = ((), (), s32[]{:S(2)}) async-start(), calls=%async_computation.5 | async-start | bytes 2654208 | tf_op jit(solution)/shard_map/reduce_scatter | solution.py:96
  141.1 9.2 %copy-start.1 = (f32[512,1536]{1,0:T(8,128)S(1)}, f32[512,1536]{1,0:T(8,128)}, u32[]{:S(2)}) copy-start(f32[512,1536]{1,0:T(8,128)} %copy-done) | copy-start | bytes 9437188
  150.3 0.9 copy-start.9
  150.3 1.4 copy-start.3
  150.8 0.9 copy-start.10
  155.5 18.4 %copy-start.8 = (bf16[1,512,768]{2,1,0:T(8,128)(2,1)S(1)}, bf16[1,512,768]{2,1,0:T(8,128)(2,1)}, u32[]{:S(2)}) copy-start(bf16[1,512,768]{2,1,0:T(8,128)(2,1)} %param.13) | copy-start | bytes 2359300
  173.8 1.5 copy-start.7
  173.8 2.0 copy-start.12
Sparse Core Ops, SparseCore 0:
  10.1 68.8 all-gather.3
  81.1 44.8 all-gather.5
  137.7 42.8 reduce-scatter.9
  183.5 46.9 reduce-scatter.7
  233.5 66.8 reduce-scatter.5
where the time goes:
time: 580 us; the launch traced here: 576 us
  blocking collectives  320 us (55%)
  waiting for transfers between devices  184 us (32%)
  other arithmetic  26.7 us (5%)
  matrix products  20.9 us (4%)
  between operations  16.2 us (3%)
  local copies, waits for them, and re-layouts  6.83 us (1%)
    psum x1, blocking collectives, body(): lax.psum((slices[0], slices[1], slices[2], slices[3]), 'replica')  266 us
    reduce_scatter x1, waiting for transfers between devices, body(): lax.psum_scatter(up_part.astype(jnp.bfloat16), 'shard', scatter_dimension...  69.9 us
    reduce_scatter x1, waiting for transfers between devices, body(): lax.psum_scatter(down_part.astype(jnp.bfloat16), 'shard', scatter_dimensi...  49.1 us
    all_gather x1, waiting for transfers between devices, body(): down_full = lax.all_gather(down_weight, 'shard', axis=1, tiled=True)  33.9 us
    unnamed x2, blocking collectives  31.4 us
    all_gather x1, waiting for transfers between devices, body(): lax.all_gather(up_weight, 'shard', axis=0, tiled=True)  27.2 us
    all_gather x1, blocking collectives, body(): lax.all_gather(conv_kernel, 'shard', axis=1, tiled=True)  22.9 us
  transfers between devices with their start and end apart: 5, of which 5 were waited for; matrix products, arithmetic and copies ran while one was open for 6% of the time, Pallas kernels for 0%

commit v1 on v0

v1 whole, which is shorter than its diff:
```python
import jax
import jax.numpy as jnp
from jax import lax
from jax.experimental import pallas as pl
from jax.experimental.pallas import tpu as pltpu
from jax.sharding import PartitionSpec as P

EPS = 1e-05
WIDE = 2432
CUT = 1280
MESH = pl.DeviceIdType.MESH


def place():
    rep, sh = lax.axis_index("replica"), lax.axis_index("shard")
    z, y_hi, core = rep // 4, (rep // 2) % 2, rep % 2
    x, y_lo = sh // 2, sh % 2
    return x, y_hi * 2 + y_lo, z, core


def device(x, y, z, core):
    return ((z * 2 + y // 2) * 2 + core, x * 2 + y % 2)


def greet(partners):
    barrier = pltpu.get_barrier_semaphore()
    for partner in partners:
        pl.semaphore_signal(barrier, inc=1, device_id=partner, device_id_type=MESH)
    pl.semaphore_wait(barrier, len(partners))


def gather_kernel(w_ref, out_ref, local_sem, send_sem, recv_sem):
    x, y, z, core = place()
    y_lo = y % 2
    xp, xm, x2 = (x + 1) % 4, (x + 3) % 4, (x + 2) % 4
    yp, ym = (y + 1) % 4, (y + 3) % 4
    to_xp, to_xm = device(xp, y, z, core), device(xm, y, z, core)
    to_yp, to_ym = device(x, yp, z, core), device(x, ym, z, core)
    to_sib = device(x, y, z, 1 - core)
    greet([to_xp, to_xm, to_yp, to_ym, to_sib])

    def rows(bx, byl):
        return pl.ds(pl.multiple_of((bx * 2 + byl) * 96 + core * 48, 16), 48)

    LO, HI, ALL = pl.ds(0, CUT), pl.ds(CUT, WIDE - CUT), pl.ds(0, WIDE)
    own = pl.multiple_of((x * 2 + y_lo) * 96, 16)
    local = pltpu.make_async_copy(w_ref, out_ref.at[pl.ds(own, 96)], local_sem)
    local.start()
    mine = pl.ds(pl.multiple_of(core * 48, 16), 48)
    sent = []

    def send(index, bx, byl, cols, target, own_block=False):
        dst = out_ref.at[rows(bx, byl), cols]
        src = w_ref.at[mine, cols] if own_block else dst
        copy = pltpu.make_async_remote_copy(
            src_ref=src, dst_ref=dst, send_sem=send_sem.at[index], recv_sem=recv_sem.at[index],
            device_id=target, device_id_type=MESH)
        copy.start()
        sent.append(copy)

    def arrive(index, bx, byl, cols):
        dst = out_ref.at[rows(bx, byl), cols]
        pltpu.make_async_remote_copy(
            src_ref=dst, dst_ref=dst, send_sem=send_sem.at[index], recv_sem=recv_sem.at[index],
            device_id=to_sib, device_id_type=MESH).wait_recv()

    oth = 1 - y_lo
    send(0, x, y_lo, ALL, to_xp, True)
    send(1, x, y_lo, ALL, to_xm, True)
    send(4, x, y_lo, LO, to_yp, True)
    send(8, x, y_lo, HI, to_ym, True)
    arrive(0, xm, y_lo, ALL)
    send(2, xm, y_lo, LO, to_xp)
    send(5, xm, y_lo, LO, to_yp)
    send(9, xm, y_lo, HI, to_ym)
    arrive(1, xp, y_lo, ALL)
    send(3, xp, y_lo, HI, to_xm)
    send(6, xp, y_lo, LO, to_yp)
    send(10, xp, y_lo, HI, to_ym)
    send(12, xm, y_lo, ALL, to_sib)
    send(13, xp, y_lo, ALL, to_sib)
    arrive(4, x, oth, LO)
    send(16, x, oth, LO, to_sib)
    arrive(8, x, oth, HI)
    send(20, x, oth, HI, to_sib)
    arrive(2, x2, y_lo, LO)
    send(7, x2, y_lo, LO, to_yp)
    send(14, x2, y_lo, LO, to_sib)
    arrive(3, x2, y_lo, HI)
    send(11, x2, y_lo, HI, to_ym)
    send(15, x2, y_lo, HI, to_sib)
    for k, bx in ((1, xm), (2, xp), (3, x2)):
        arrive(4 + k, bx, oth, LO)
        send(16 + k, bx, oth, LO, to_sib)
        arrive(8 + k, bx, oth, HI)
        send(20 + k, bx, oth, HI, to_sib)

    def sib_rows(bx, byl):
        return pl.ds(pl.multiple_of((bx * 2 + byl) * 96 + (1 - core) * 48, 16), 48)

    def arrive_sib(index, bx, byl, cols):
        dst = out_ref.at[sib_rows(bx, byl), cols]
        pltpu.make_async_remote_copy(
            src_ref=dst, dst_ref=dst, send_sem=send_sem.at[index], recv_sem=recv_sem.at[index],
            device_id=to_sib, device_id_type=MESH).wait_recv()

    arrive_sib(12, xm, y_lo, ALL)
    arrive_sib(13, xp, y_lo, ALL)
    arrive_sib(14, x2, y_lo, LO)
    arrive_sib(15, x2, y_lo, HI)
    for k, bx in ((0, x), (1, xm), (2, xp), (3, x2)):
        arrive_sib(16 + k, bx, oth, LO)
        arrive_sib(20 + k, bx, oth, HI)
    for copy in sent:
        copy.wait_send()
    local.wait()


def gather_weights(packed):
    return pl.pallas_call(
        gather_kernel,
        out_shape=jax.ShapeDtypeStruct((768, WIDE), jnp.bfloat16),
        in_specs=[pl.BlockSpec(memory_space=pltpu.VMEM)],
        out_specs=pl.BlockSpec(memory_space=pltpu.VMEM),
        scratch_shapes=[
            pltpu.SemaphoreType.DMA,
            pltpu.SemaphoreType.DMA((24,)),
            pltpu.SemaphoreType.DMA((24,)),
        ],
        compiler_params=pltpu.CompilerParams(collective_id=0, has_side_effects=True),
        name="gather_weights",
    )(packed)


def add_rows(rows, step, dst, terms):
    def one(i, carry):
        at = pl.ds(pl.multiple_of(i * step, 16), step)
        total = terms[0](at).astype(jnp.float32)
        for term in terms[1:]:
            total = total + term(at).astype(jnp.float32)
        dst(at, total)
        return carry

    lax.fori_loop(0, rows // step, one, 0)


def reduce_kernel(factor, g_ref, out_ref, cr, cs, xr, xq, xs, yr, yq, zs, zr, fin,
                  send_sem, recv_sem, zsend, zrecv, asend, arecv):
    x, y, z, core = place()
    y_lo, y_hi = y % 2, y // 2
    xp, xm, x2 = (x + 1) % 4, (x + 3) % 4, (x + 2) % 4
    yp, ym, y2 = (y + 1) % 4, (y + 3) % 4, (y + 2) % 4
    to_xp, to_xm = device(xp, y, z, core), device(xm, y, z, core)
    to_yp, to_ym = device(x, yp, z, core), device(x, ym, z, core)
    to_y2 = device(x, y2, z, core)
    to_sib = device(x, y, z, 1 - core)

    barrier = pltpu.get_barrier_semaphore()
    for partner in (to_xp, to_xm, to_yp, to_ym, to_y2, to_sib):
        pl.semaphore_signal(barrier, inc=1, device_id=partner, device_id_type=MESH)

    def hello(d, carry):
        pl.semaphore_signal(barrier, inc=1, device_id=device(x, y, (z + d) % 16, core), device_id_type=MESH)
        return carry

    lax.fori_loop(1, 16, hello, 0)
    pl.semaphore_wait(barrier, 21)
    sent = []

    def copy(index, src, dst, target):
        return pltpu.make_async_remote_copy(
            src_ref=src, dst_ref=dst, send_sem=send_sem.at[index], recv_sem=recv_sem.at[index],
            device_id=target, device_id_type=MESH)

    def send(index, src, dst, target):
        c = copy(index, src, dst, target)
        c.start()
        sent.append(c)

    def arrive(index, dst):
        copy(index, dst, dst, to_sib).wait_recv()

    order = (x2, xp, xm, x)
    for k, bx in enumerate(order):
        send(k, g_ref.at[bx, :, 1 - core], cr.at[bx], to_sib)
    def core_sum(k):
        bx = order[k]
        arrive(k, cr.at[bx])
        for j in range(2):
            def put(at, v):
                cs[bx, j, at, :] = v.astype(jnp.bfloat16)
            add_rows(896, 128, put, [lambda at: g_ref[bx, j, core, at, :], lambda at: cr[bx, j, at, :]])

    core_sum(0)
    send(4, cs.at[x2, 0], xq.at[0], to_xp)
    send(5, cs.at[x2, 1], xq.at[1], to_xm)
    core_sum(1)
    send(6, cs.at[xp, 1], xr.at[0, 1], to_xp)
    core_sum(2)
    send(7, cs.at[xm, 0], xr.at[1, 0], to_xm)
    arrive(4, xq.at[0])

    def put_p(at, v):
        cs[xp, 0, at, :] = v.astype(jnp.bfloat16)

    add_rows(896, 128, put_p, [lambda at: cs[xp, 0, at, :], lambda at: xq[0, at, :]])
    send(8, cs.at[xp, 0], xr.at[0, 0], to_xp)
    arrive(5, xq.at[1])

    def put_m(at, v):
        cs[xm, 1, at, :] = v.astype(jnp.bfloat16)

    add_rows(896, 128, put_m, [lambda at: cs[xm, 1, at, :], lambda at: xq[1, at, :]])
    send(9, cs.at[xm, 1], xr.at[1, 1], to_xm)
    core_sum(3)
    arrive(6, xr.at[0, 1])
    arrive(7, xr.at[1, 0])
    arrive(8, xr.at[0, 0])
    arrive(9, xr.at[1, 1])
    for j in range(2):
        def put(at, v):
            xs[j, at, :] = v.astype(jnp.bfloat16)
        add_rows(896, 128, put, [lambda at: cs[x, j, at, :], lambda at: xr[0, j, at, :], lambda at: xr[1, j, at, :]])

    def part(yy, half, rows=224):
        return xs.at[yy % 2, pl.ds(pl.multiple_of((yy // 2) * 448 + half * 224, 16), rows)]

    send(10, part(y2, 0), yq.at[0], to_yp)
    send(11, part(y2, 1), yq.at[1], to_ym)
    send(12, part(yp, 1), yr.at[0, 1], to_yp)
    send(13, part(ym, 0), yr.at[1, 0], to_ym)
    arrive(10, yq.at[0])
    dst_p = part(yp, 0)

    def put_yp(at, v):
        dst_p[at, :] = v.astype(jnp.bfloat16)

    add_rows(224, 32, put_yp, [lambda at: dst_p[at, :], lambda at: yq[0, at, :]])
    send(14, part(yp, 0), yr.at[0, 0], to_yp)
    arrive(11, yq.at[1])
    dst_m = part(ym, 1)

    def put_ym(at, v):
        dst_m[at, :] = v.astype(jnp.bfloat16)

    add_rows(224, 32, put_ym, [lambda at: dst_m[at, :], lambda at: yq[1, at, :]])
    send(15, part(ym, 1), yr.at[1, 1], to_ym)
    arrive(12, yr.at[0, 1])
    arrive(13, yr.at[1, 0])
    arrive(14, yr.at[0, 0])
    arrive(15, yr.at[1, 1])
    zs[pl.ds(448, 64), :] = jnp.zeros((64, 128), jnp.bfloat16)
    for half in range(2):
        mine = part(y, half)

        def put(at, v):
            zs[pl.ds(pl.multiple_of(half * 224 + at.start, 16), 32), :] = v.astype(jnp.bfloat16)

        add_rows(224, 32, put, [lambda at: mine[at, :], lambda at: yr[0, half, at, :], lambda at: yr[1, half, at, :]])

    def piece(p):
        return pl.ds(pl.multiple_of(p * 32, 32), 32)

    def z_copy(d):
        to = (z + d) % 16
        return pltpu.make_async_remote_copy(
            src_ref=zs.at[piece(to)], dst_ref=zr.at[d], send_sem=zsend.at[d], recv_sem=zrecv.at[d],
            device_id=device(x, y, to, core), device_id_type=MESH)

    def z_start(d, carry):
        z_copy(d).start()
        return carry

    lax.fori_loop(1, 16, z_start, 0)

    def z_add(d, total):
        z_copy(d).wait_recv()
        return total + zr[d].astype(jnp.float32)

    total = lax.fori_loop(1, 16, z_add, zs[piece(z), :].astype(jnp.float32))
    mine_at = fin.at[core, y_hi]
    mine_at[piece(z), :] = total.astype(jnp.bfloat16)

    def a_copy(d, p):
        at = fin.at[core, y_hi, piece(p)]
        return pltpu.make_async_remote_copy(
            src_ref=at, dst_ref=at, send_sem=asend.at[d], recv_sem=arecv.at[d],
            device_id=device(x, y, (z + d) % 16, core), device_id_type=MESH)

    def a_start(d, carry):
        a_copy(d, z).start()
        return carry

    lax.fori_loop(1, 16, a_start, 0)

    def a_wait(d, carry):
        a_copy(d, (z + 16 - d) % 16).wait_recv()
        return carry

    lax.fori_loop(1, 16, a_wait, 0)
    both = fin.at[core, y_hi, pl.ds(0, 448)]
    send(16, both, both, to_y2)
    send(17, both, both, to_sib)
    far = fin.at[core, 1 - y_hi, pl.ds(0, 448)]
    arrive(16, far)
    send(18, far, far, to_sib)

    def z_done(d, carry):
        z_copy(d).wait_send()
        a_copy(d, z).wait_send()
        return carry

    lax.fori_loop(1, 16, z_done, 0)
    arrive(17, fin.at[1 - core, y_hi, pl.ds(0, 448)])
    arrive(18, fin.at[1 - core, 1 - y_hi, pl.ds(0, 448)])
    for c in range(2):
        for h in range(2):
            def put(at, v):
                out_ref[c, h, at, :] = v * factor
            add_rows(448, 64, put, [lambda at: fin[c, h, at, :]])
    for c in sent:
        c.wait_send()


def reduce_parts(packed, factor):
    bf = jnp.bfloat16
    return pl.pallas_call(
        lambda *refs: reduce_kernel(factor, *refs),
        out_shape=jax.ShapeDtypeStruct((2, 2, 448, 128), jnp.float32),
        in_specs=[pl.BlockSpec(memory_space=pltpu.VMEM)],
        out_specs=pl.BlockSpec(memory_space=pltpu.VMEM),
        scratch_shapes=[
            pltpu.VMEM((4, 2, 896, 128), bf),
            pltpu.VMEM((4, 2, 896, 128), bf),
            pltpu.VMEM((2, 2, 896, 128), bf),
            pltpu.VMEM((2, 896, 128), bf),
            pltpu.VMEM((2, 896, 128), bf),
            pltpu.VMEM((2, 2, 224, 128), bf),
            pltpu.VMEM((2, 224, 128), bf),
            pltpu.VMEM((512, 128), bf),
            pltpu.VMEM((16, 32, 128), bf),
            pltpu.VMEM((2, 2, 512, 128), bf),
            pltpu.SemaphoreType.DMA((19,)),
            pltpu.SemaphoreType.DMA((19,)),
            pltpu.SemaphoreType.DMA((16,)),
            pltpu.SemaphoreType.DMA((16,)),
            pltpu.SemaphoreType.DMA((16,)),
            pltpu.SemaphoreType.DMA((16,)),
        ],
        compiler_params=pltpu.CompilerParams(collective_id=1, has_side_effects=True),
        name="reduce_parts",
    )(packed)


def tiles(array, columns):
    return array.reshape(8, 12, 8, columns, 128).transpose(0, 1, 3, 2, 4).reshape(8, 12 * columns, 8, 128)


def untiles(array, columns):
    return array.reshape(12, columns, 8, 128).transpose(0, 2, 1, 3).reshape(96, columns * 128)


def normalize(inputs):
    average = jnp.mean(inputs, axis=1, keepdims=True)
    centred = inputs - average
    inv_std = lax.rsqrt(jnp.mean(centred * centred, axis=1, keepdims=True) + EPS)
    return (centred * inv_std, inv_std)


def depthwise(signal, taps_f, front, back):
    frames = signal.shape[1]
    padded = jnp.pad(signal, ((0, 0), (front, back), (0, 0)))
    total = jnp.zeros_like(signal)
    for offset in range(taps_f.shape[0]):
        total = total + taps_f[offset] * padded[:, offset : offset + frames]
    return total


def tap_grads(grad, signal, front, back):
    frames = signal.shape[1]
    padded = jnp.pad(signal, ((0, 0), (front, back), (0, 0)))
    return jnp.stack(
        [
            jnp.sum(grad * padded[:, offset : offset + frames], axis=(0, 1))
            for offset in range(front + back + 1)
        ]
    )


def body(frames_in, lengths, up_weight, norm_gain, conv_kernel, down_weight, cotangent):
    utts, frames, width = frames_in.shape
    chans = up_weight.shape[1] // 2
    count_taps = conv_kernel.shape[0]
    front = count_taps // 2
    back = count_taps - 1 - front
    row_count = utts * frames
    bf = jnp.bfloat16
    packed = jnp.concatenate(
        [up_weight, down_weight.T, conv_kernel.T, norm_gain[:, None], jnp.zeros((96, 95), bf)], axis=1
    )
    full = gather_weights(packed)
    up_full = full[:, :1536]
    down_t = full[:, 1536:2304]
    small = full[:, 2304:].T
    taps_bf, gain_bf = small[:32], small[32]

    live = (jnp.arange(frames, dtype=jnp.int32)[None, :] < lengths[:, None]).astype(jnp.float32)
    live_col = live.reshape(row_count, 1)
    inputs = frames_in.reshape(row_count, width).astype(jnp.float32)
    normed, inv_std = normalize(inputs)
    gain_f = gain_bf.astype(jnp.float32)
    scaled = (normed * gain_f).astype(bf)
    projected = jnp.dot(scaled, up_full, preferred_element_type=jnp.float32)
    values_half = projected[:, :chans]
    gate_sig = jax.nn.sigmoid(projected[:, chans:])
    gated = (values_half * gate_sig * live_col).astype(bf)
    taps_f = taps_bf.astype(jnp.float32)
    gated_f = gated.astype(jnp.float32).reshape(utts, frames, chans)
    filtered = depthwise(gated_f, taps_f, front, back).reshape(row_count, chans)
    activated = (jax.nn.silu(filtered) * live_col).astype(bf)
    upstream = cotangent.reshape(row_count, width)
    mixed = lax.dot_general(
        activated, down_t, (((1,), (1,)), ((), ())), preferred_element_type=jnp.float32
    )
    d_act = jnp.dot(upstream, down_t, preferred_element_type=jnp.float32)
    result = (inputs + mixed).astype(bf)
    down_part = lax.dot_general(
        upstream, activated, (((0,), (0,)), ((), ())), preferred_element_type=jnp.float32
    )
    factor = 1.0 / float(utts * 512 * frames) ** 0.5
    filt_sig = jax.nn.sigmoid(filtered)
    d_filt = d_act * live_col * filt_sig * (1.0 + filtered * (1.0 - filt_sig))
    d_filt3 = d_filt.reshape(utts, frames, chans)
    kernel_part = tap_grads(d_filt3, gated_f, front, back)
    d_gated = depthwise(d_filt3, taps_f[::-1], back, front).reshape(row_count, chans) * live_col
    d_proj = jnp.concatenate(
        [d_gated * gate_sig, d_gated * values_half * gate_sig * (1.0 - gate_sig)], axis=1
    ).astype(bf)
    up_part = lax.dot_general(
        scaled, d_proj, (((0,), (0,)), ((), ())), preferred_element_type=jnp.float32
    )
    d_scaled = lax.dot_general(
        d_proj, up_full, (((1,), (1,)), ((), ())), preferred_element_type=jnp.float32
    )
    gain_part = jnp.sum(d_scaled * normed, axis=0)
    d_normed = d_scaled * gain_f
    d_inputs = inv_std * (
        d_normed
        - jnp.mean(d_normed, axis=1, keepdims=True)
        - normed * jnp.mean(d_normed * normed, axis=1, keepdims=True)
    )
    grad_in = (upstream.astype(jnp.float32) + d_inputs).astype(bf)

    taps_tiles = jnp.pad(
        kernel_part.astype(bf).reshape(32, 8, 96).transpose(1, 0, 2), ((0, 0), (0, 0), (0, 32))
    ).reshape(8, 4, 8, 128)
    gain_tiles = jnp.pad(
        gain_part.astype(bf).reshape(8, 1, 1, 96), ((0, 0), (0, 3), (0, 7), (0, 32))
    )
    parts = jnp.concatenate(
        [tiles(up_part.astype(bf), 12), tiles(down_part.astype(bf), 6), taps_tiles, gain_tiles], axis=1
    ).reshape(4, 2, 2, 896, 128)
    total = reduce_parts(parts, factor).reshape(224, 8, 128)
    up_total = untiles(total[:144], 12)
    down_total = untiles(total[144:216], 6).T
    kernel_total = total[216:220].reshape(32, 128)[:, :96]
    gain_total = total[220, 0, :96]
    return (
        result.reshape(utts, frames, width),
        grad_in.reshape(utts, frames, width),
        up_total,
        gain_total,
        kernel_total,
        down_total,
    )


def solution(mesh):
    return jax.shard_map(
        body,
        mesh=mesh,
        in_specs=(
            P(("replica", "shard"), None, None),
            P(("replica", "shard")),
            P("shard", None),
            P("shard"),
            P(None, "shard"),
            P(None, "shard"),
            P(("replica", "shard"), None, None),
        ),
        out_specs=(
            P(("replica", "shard"), None, None),
            P(("replica", "shard"), None, None),
            P("shard", None),
            P("shard"),
            P(None, "shard"),
            P(None, "shard"),
        ),
        check_vma=False,
    )
```

time: 580 us -> 161 us (0.28)
  blocking collectives: 320 us -> 0 us
  waiting for transfers between devices: 184 us -> 0 us
  Pallas kernels: 0 us -> 95.2 us
  local copies, waits for them, and re-layouts: 6.83 us -> 22.8 us
  between operations: 16.2 us -> 1.82 us
  matrix products: 20.9 us -> 13.4 us
    psum x1 -> x0, blocking collectives: 266 us -> none  [body(): lax.psum((slices[0], slices[1], slices[2], slices[3]), 'replica')]
    reduce_scatter x2 -> x0, waiting for transfers between devices: 119 us -> none  [the longest x1 69.9 us: body(): lax.psum_scatter(up_part.astype(jnp.bfloat16), 'shard', scatter_dimension...]
    pallas_call x0 -> x2, Pallas kernels: none -> 95.2 us  [the longest x1 68.4 us: reduce_parts(): pl.pallas_call(lambda *refs: reduce_kernel(factor, *refs), out_shape=jax....]
    all_gather x2 -> x0, waiting for transfers between devices: 61 us -> none  [the longest x1 33.9 us: body(): down_full = lax.all_gather(down_weight, 'shard', axis=1, tiled=True)]
    unnamed x2 -> x0, blocking collectives: 31.4 us -> none
    all_gather x1 -> x0, blocking collectives: 22.9 us -> none  [body(): lax.all_gather(conv_kernel, 'shard', axis=1, tiled=True)]
    slice x2, local copies, waits for them, and re-layouts: 0.28 us -> 6.56 us  [depthwise(): total = total + taps_f[offset] * padded[:, offset:offset + frames]]
  transfers between devices with their start and end apart: 5 -> 0, of which waited for: 5 -> 0; matrix products, arithmetic and copies ran while one was open for 6% -> 0% of each run, Pallas kernels for 0% -> 0%
where the time goes in v1:
time: 161 us
  Pallas kernels  95.2 us (59%)
  other arithmetic  27.6 us (17%)
  local copies, waits for them, and re-layouts  22.8 us (14%)
  matrix products  13.4 us (8%)
  between operations  1.82 us (1%)
    pallas_call x1, Pallas kernels, reduce_parts(): pl.pallas_call(lambda *refs: reduce_kernel(factor, *refs), out_shape=jax....  68.4 us
    pallas_call x1, Pallas kernels, gather_weights(): pl.pallas_call(gather_kernel, out_shape=jax.ShapeDtypeStruct((768, WIDE),...  26.7 us
    another operation x2, other arithmetic  9.67 us
    add x1, other arithmetic, depthwise(): total = total + taps_f[offset] * padded[:, offset:offset + frames]  6.66 us
    slice x2, local copies, waits for them, and re-layouts, depthwise(): total = total + taps_f[offset] * padded[:, offset:offset + frames]  6.56 us
    dot_general x1, matrix products, body(): d_act = jnp.dot(upstream, down_t, preferred_element_type=jnp.float32)  5.68 us
    reduce_sum x2, other arithmetic, tap_grads(): jnp.sum(grad * padded[:, offset:offset + frames], axis=(0, 1))  4.34 us
    unnamed x72, local copies, waits for them, and re-layouts  3.77 us

profile of v1, /device:TPU:1, one launch (start us, length us, event | category | flops | bytes accessed | tf_op | source)
XLA Modules:
  0.0 160.8 jit_solution(1456902945409279748)
XLA Ops:
  1.4 1.3 convert_reduce_fusion
  2.7 1.5 fusion.21
  5.4 26.7 %gather_weights.1 = bf16[768,2432]{1,0:T(8,128)(2,1)} custom-call(bf16[96,2432]{1,0:T(8,128)(2,1)} %concatenate.12.w_ref), custom_call_target="tpu_custom_call" | custom-call | tf_op jit(solution)/shard_map/gather_weights/pallas_call | solution.py:120
  33.3 2.7 %slice_reduce_fusion.30 = (f32[768]{0:T(1024)S(1)}, f32[768]{0:T(1024)S(1)}, f32[768]{0:T(1024)S(1)}, f32[768]{0:T(1024)S(1)}, f32[768]{0:T(1024)S(1)}, /*index=...) fusion(f32[32,768]{0,1:T(8,128)S(1)} %slice_convert_fusion), kind=kLoop, calls=%fused_computation.161 | loop fusion | bytes 79872 | tf_op jit(solution)/shard_map/slice | solution.py:375
  36.1 3.8 %slice_reduce_fusion.31 = (f32[768]{0:T(1024)S(1)}, f32[768]{0:T(1024)S(1)}, f32[768]{0:T(1024)S(1)}, f32[768]{0:T(1024)S(1)}, f32[768]{0:T(1024)S(1)}, /*index=...) fusion(f32[32,768]{0,1:T(8,128)S(1)} %slice_convert_fusion), kind=kLoop, calls=%fused_computation.162 | loop fusion | bytes 116736 | tf_op jit(solution)/shard_map/slice | solution.py:375
  39.9 1.5 fusion.4
  41.9 1.2 copy-done
  43.1 6.7 %fusion.39 = f32[1,512,768]{2,1,0:T(8,128)S(1)} fusion(bf16[512,768]{1,0:T(8,128)(2,1)S(1)} %get-tuple-element.75, f32[768]{0:T(1024)S(1)} %get-tuple-element.41, f32[768]{0:T(1024)S(1)} %get-tuple-element.42, f32[768]{0:T(1024)S(1)} %get-tuple-element.43, f32[768]{0:T(1024)S(1)} %get-tuple-element.44, f32[768]{0:T(1024)S(1)} %get-tuple-element.45, ...), kind=kLoop, calls=%fused_computation.46 | loop fusion | flops 25165824 | bytes 4030464 | tf_op jit(solution)/shard_map/add | solution.py:375
  49.8 1.9 %fusion.69 = bf16[1,512,768]{2,1,0:T(8,128)(2,1)} fusion(bf16[1,512,768]{2,1,0:T(8,128)(2,1)S(1)} %copy-done.2, bf16[768,2432]{1,0:T(8,128)(2,1)S(1)} %copy-done.7, f32[1,512,768]{2,1,0:T(8,128)S(1)} %fusion.39, f32[512]{0:T(512)S(1)} %fusion.79), kind=kOutput, calls=%fused_computation.122 | convolution fusion | flops 607518720 | bytes 4327424 | tf_op jit(solution)/shard_map/dot_general | solution.py:422
  51.8 1.0 fusion.68
  52.8 1.5 copy.18
  54.3 5.7 %multiply_reduce_fusion.1 = (bf16[768]{0:T(1024)(128)(2,1)S(1)}, bf16[768]{0:T(1024)(128)(2,1)S(1)}, bf16[768]{0:T(1024)(128)(2,1)S(1)}, bf16[768]{0:T(1024)(128...) fusion(f32[1,512,768]{2,1,0:T(8,128)S(1)} %get-tuple-element.74, ...), kind=kOutput, calls=%fused_computation.83 | convolution fusion | flops 617732352 | bytes 6706688 | tf_op jit(solution)/shard_map/dot_general | solution.py:425
  60.0 4.1 %multiply_reduce_fusion = (bf16[768]{0:T(1024)(128)(2,1)S(1)}, bf16[768]{0:T(1024)(128)(2,1)S(1)}, bf16[768]{0:T(1024)(128)(2,1)S(1)}, bf16[768]{0:T(1024)(128)(...) fusion(f32[1,512,768]{2,1,0:T(8,128)S(1)} %get-tuple-element.74, ...), kind=kLoop, calls=%fused_computation.82 | loop fusion | flops 14141952 | bytes 3173376 | tf_op jit(solution)/shard_map/reduce_sum | solution.py:384
  67.5 9.2 %multiply_convert_fusion.2 = (bf16[512,768]{1,0:T(8,128)(2,1)S(1)}, f32[512,768]{1,0:T(8,128)S(1)}) fusion(f32[512,1536]{1,0:T(8,128)} %copy-done, f32[512]{0:T(512)S(1)} %fusion.79, f32[768]{0:T(1024)S(1)} %get-tuple-element.40, f32[768]{0:T(1024)S(1)} %get-tuple-element.59, f32[768]{0:T(1024)S(1)} %get-tuple-element.71, f32[768]{0:T(1024)S(1)} %get-tuple-element.70, ...), kind=kLoop, calls=%fused_computation.115 | loop fusion | flops 27131904 | bytes 7178240 | tf_op jit(solution)/shard_map/convert.65
  78.2 1.2 copy-done.8
  79.3 1.7 %fusion.20 = (bf16[768]{0:T(1024)(128)(2,1)S(1)}, f32[512]{0:T(512)S(1)}, f32[512]{0:T(512)S(1)}, f32[512,768]{1,0:T(8,128)S(1)}) fusion(bf16[1,512,768]{2,1,0:T(8,128)(2,1)S(1)} %copy-done.3, f32[512]{0:T(512)S(1)} %add_rsqrt_fusion, f32[512]{0:T(512)S(1)} %broadcast_multiply_fusion.2, f32[768]{0:T(1024)S(1)} %convert_reduce_fusion.1, ...), kind=kOutput, calls=%fused_computation.27 | convolution fusion | flops 1214642432 | bytes 6305280 | tf_op jit(solution)/shard_map/dot_general | solution.py:442
  81.2 1.5 fusion.72
  82.7 1.6 convolution_convert_fusion
  84.3 1.9 %fusion.1 = bf16[8,224,8,128]{3,2,1,0:T(8,128)(2,1)} fusion(bf16[8,1,1,96]{3,2,1,0:T(2,128)(2,1)S(1)} %convert_element_type.98, bf16[8,4,8,128]{3,2,1,0:T(8,128)(2,1)S(1)} %copy.19, bf16[8,72,8,128]{3,2,1,0:T(8,128)(2,1)S(1)} %bitcast.234, bf16[8,144,8,128]{3,2,1,0:T(8,128)(2,1)S(1)} %bitcast.239), kind=kLoop, calls=%fused_computation.2 | loop fusion | flops 18350080 | bytes 7276032 | tf_op jit(solution)/shard_map/concatenate | solution.py:460
  86.2 68.4 %reduce_parts.1 = f32[2,2,448,128]{3,2,1,0:T(8,128)} custom-call(bf16[4,2,2,896,128]{4,3,2,1,0:T(8,128)(2,1)} %bitcast.233), custom_call_target="tpu_custom_call" | custom-call | tf_op jit(solution)/shard_map/reduce_parts/pallas_call | solution.py:327
  154.7 1.2 slice_bitcast_fusion.2
  155.9 1.3 slice_bitcast_fusion.1
  157.2 1.7 %slice.562 = f32[72,8,128]{2,1,0:T(8,128)} slice(f32[224,8,128]{2,1,0:T(8,128)} %bitcast.237), slice={[144:216], [0:8], [0:128]} | slice | bytes 589824 | tf_op jit(solution)/shard_map/slice | solution.py:465
  158.9 1.9 %slice.558 = f32[144,8,128]{2,1,0:T(8,128)} slice(f32[224,8,128]{2,1,0:T(8,128)} %bitcast.238), slice={[0:144], [0:8], [0:128]} | slice | bytes 1179648 | tf_op jit(solution)/shard_map/slice | solution.py:464
  (119 shorter events, 7.6 us)
Async XLA Ops:
  0.6 3.8 %copy-start.17 = (bf16[768,96]{0,1:T(8,128)(2,1)S(1)}, bf16[768,96]{0,1:T(8,128)(2,1)}, u32[]{:S(2)}) copy-start(bf16[768,96]{0,1:T(8,128)(2,1)} %param.12) | copy-start | bytes 442372
  0.6 3.7 %copy-start.18 = (bf16[32,96]{1,0:T(8,128)(2,1)S(1)}, bf16[32,96]{1,0:T(8,128)(2,1)}, u32[]{:S(2)}) copy-start(bf16[32,96]{1,0:T(8,128)(2,1)} %param.11) | copy-start | bytes 18436
  0.7 3.6 %copy-start.19 = (bf16[96]{0:T(256)(128)(2,1)S(1)}, bf16[96]{0:T(256)(128)(2,1)}, u32[]{:S(2)}) copy-start(bf16[96]{0:T(256)(128)(2,1)} %param.10) | copy-start | bytes 580
  0.7 3.8 %copy-start.16 = (bf16[96,1536]{1,0:T(8,128)(2,1)S(1)}, bf16[96,1536]{1,0:T(8,128)(2,1)}, u32[]{:S(2)}) copy-start(bf16[96,1536]{1,0:T(8,128)(2,1)} %param.9) | copy-start | bytes 884740
  36.1 3.9 %copy-start.2 = (bf16[1,512,768]{2,1,0:T(8,128)(2,1)S(1)}, bf16[1,512,768]{2,1,0:T(8,128)(2,1)}, u32[]{:S(2)}) copy-start(bf16[1,512,768]{2,1,0:T(8,128)(2,1)} %param.7) | copy-start | bytes 2359300
  36.1 3.9 %copy-start.7 = (bf16[768,2432]{1,0:T(8,128)(2,1)S(1)}, bf16[768,2432]{1,0:T(8,128)(2,1)}, u32[]{:S(2)}) copy-start(bf16[768,2432]{1,0:T(8,128)(2,1)} %gather_weights.1) | copy-start | bytes 11206660
  41.4 1.7 %copy-start = (f32[512,1536]{1,0:T(8,128)}, f32[512,1536]{1,0:T(8,128)S(1)}, u32[]{:S(2)}) copy-start(f32[512,1536]{1,0:T(8,128)S(1)} %fusion.4) | copy-start | bytes 9437188
  43.1 6.7 %copy-start.4 = (bf16[512,768]{1,0:T(8,128)(2,1)}, bf16[512,768]{1,0:T(8,128)(2,1)S(1)}, u32[]{:S(2)}) copy-start(bf16[512,768]{1,0:T(8,128)(2,1)S(1)} %get-tuple-element.75) | copy-start | bytes 2359300
  49.8 2.0 %copy-start.9 = (f32[1,512,768]{2,1,0:T(8,128)}, f32[1,512,768]{2,1,0:T(8,128)S(1)}, u32[]{:S(2)}) copy-start(f32[1,512,768]{2,1,0:T(8,128)S(1)} %fusion.39) | copy-start | bytes 4718596
  49.8 2.0 %copy-start.10 = (bf16[1,512,768]{2,1,0:T(8,128)(2,1)S(1)}, bf16[1,512,768]{2,1,0:T(8,128)(2,1)}, u32[]{:S(2)}) copy-start(bf16[1,512,768]{2,1,0:T(8,128)(2,1)} %param.13) | copy-start | bytes 2359300
  60.0 4.1 %copy-start.5 = (bf16[512,768]{1,0:T(8,128)(2,1)S(1)}, bf16[512,768]{1,0:T(8,128)(2,1)}, u32[]{:S(2)}) copy-start(bf16[512,768]{1,0:T(8,128)(2,1)} %copy-done.4) | copy-start | bytes 2359300
  67.5 9.2 %copy-start.1 = (f32[512,1536]{1,0:T(8,128)S(1)}, f32[512,1536]{1,0:T(8,128)}, u32[]{:S(2)}) copy-start(f32[512,1536]{1,0:T(8,128)} %copy-done) | copy-start | bytes 9437188
  76.7 0.9 copy-start.12
  76.7 1.4 copy-start.3
  76.8 2.6 %copy-start.8 = (bf16[768,2432]{1,0:T(8,128)(2,1)S(1)}, bf16[768,2432]{1,0:T(8,128)(2,1)}, u32[]{:S(2)}) copy-start(bf16[768,2432]{1,0:T(8,128)(2,1)} %gather_weights.1) | copy-start | bytes 11206660
  79.3 1.7 %copy-start.14 = (bf16[512,768]{1,0:T(8,128)(2,1)}, bf16[512,768]{1,0:T(8,128)(2,1)S(1)}, u32[]{:S(2)}) copy-start(bf16[512,768]{1,0:T(8,128)(2,1)S(1)} %multiply_convert_fusion.1) | copy-start | bytes 2359300
  79.3 1.8 %copy-start.11 = (bf16[1,512,768]{2,1,0:T(8,128)(2,1)S(1)}, bf16[1,512,768]{2,1,0:T(8,128)(2,1)}, u32[]{:S(2)}) copy-start(bf16[1,512,768]{2,1,0:T(8,128)(2,1)} %param.13) | copy-start | bytes 2359300
  81.1 1.5 copy-start.13
  81.2 1.5 copy-start.15
  82.7 1.6 copy-start.6

commit v2 on v1

--- a/solution.py
+++ b/solution.py
@@ -1,3 +1,5 @@
+import functools
+
 import jax
 import jax.numpy as jnp
 from jax import lax
@@ -144,7 +146,7 @@
     lax.fori_loop(0, rows // step, one, 0)
 
 
-def reduce_kernel(factor, g_ref, out_ref, cr, cs, xr, xq, xs, yr, yq, zs, zr, fin,
+def reduce_kernel(factor, g_ref, up_ref, down_ref, rest_ref, cr, cs, xr, xq, xs, yr, yq, zs, zr, fin,
                   send_sem, recv_sem, zsend, zrecv, asend, arecv):
     x, y, z, core = place()
     y_lo, y_hi = y % 2, y // 2
@@ -313,11 +315,17 @@
     lax.fori_loop(1, 16, z_done, 0)
     arrive(17, fin.at[1 - core, y_hi, pl.ds(0, 448)])
     arrive(18, fin.at[1 - core, 1 - y_hi, pl.ds(0, 448)])
-    for c in range(2):
-        for h in range(2):
-            def put(at, v):
-                out_ref[c, h, at, :] = v * factor
-            add_rows(448, 64, put, [lambda at: fin[c, h, at, :]])
+    def tile(row):
+        at = row % 448
+        return fin[row // 896, (row % 896) // 448, pl.ds(at, 16), :].astype(jnp.float32) * factor
+
+    for rt in range(6):
+        for ct in range(12):
+            up_ref[pl.ds(rt * 16, 16), pl.ds(ct * 128, 128)] = tile((rt * 12 + ct) * 16)
+        for ct in range(6):
+            down_ref[pl.ds(rt * 16, 16), pl.ds(ct * 128, 128)] = tile(1152 + (rt * 6 + ct) * 16)
+    for k in range(3):
+        rest_ref[pl.ds(k * 16, 16), :] = tile(1728 + k * 16)
     for c in sent:
         c.wait_send()
 
@@ -326,9 +334,13 @@
     bf = jnp.bfloat16
     return pl.pallas_call(
         lambda *refs: reduce_kernel(factor, *refs),
-        out_shape=jax.ShapeDtypeStruct((2, 2, 448, 128), jnp.float32),
+        out_shape=(
+            jax.ShapeDtypeStruct((96, 1536), jnp.float32),
+            jax.ShapeDtypeStruct((96, 768), jnp.float32),
+            jax.ShapeDtypeStruct((48, 128), jnp.float32),
+        ),
         in_specs=[pl.BlockSpec(memory_space=pltpu.VMEM)],
-        out_specs=pl.BlockSpec(memory_space=pltpu.VMEM),
+        out_specs=(pl.BlockSpec(memory_space=pltpu.VMEM),) * 3,
         scratch_shapes=[
             pltpu.VMEM((4, 2, 896, 128), bf),
             pltpu.VMEM((4, 2, 896, 128), bf),
@@ -352,126 +364,224 @@
     )(packed)
 
 
-def tiles(array, columns):
-    return array.reshape(8, 12, 8, columns, 128).transpose(0, 1, 3, 2, 4).reshape(8, 12 * columns, 8, 128)
-
-
-def untiles(array, columns):
-    return array.reshape(12, columns, 8, 128).transpose(0, 2, 1, 3).reshape(96, columns * 128)
-
-
-def normalize(inputs):
-    average = jnp.mean(inputs, axis=1, keepdims=True)
-    centred = inputs - average
-    inv_std = lax.rsqrt(jnp.mean(centred * centred, axis=1, keepdims=True) + EPS)
-    return (centred * inv_std, inv_std)
-
-
-def depthwise(signal, taps_f, front, back):
-    frames = signal.shape[1]
-    padded = jnp.pad(signal, ((0, 0), (front, back), (0, 0)))
-    total = jnp.zeros_like(signal)
-    for offset in range(taps_f.shape[0]):
-        total = total + taps_f[offset] * padded[:, offset : offset + frames]
-    return total
-
-
-def tap_grads(grad, signal, front, back):
-    frames = signal.shape[1]
-    padded = jnp.pad(signal, ((0, 0), (front, back), (0, 0)))
-    return jnp.stack(
-        [
-            jnp.sum(grad * padded[:, offset : offset + frames], axis=(0, 1))
-            for offset in range(front + back + 1)
-        ]
+def layer_kernel(len_ref, x_ref, ct_ref, upv_ref, upg_ref, dt_ref, taps_ref, gain_ref,
+                 res_ref, gin_ref, g_ref,
+                 normed, invs, scaled, scaled_t, cot_t, vals, gsig, dact, gat, dfl, act, dpv, dpg,
+                 mixed, dsc, kacc, kall):
+    i = pl.program_id(0)
+    f32, bf = jnp.float32, jnp.bfloat16
+    length = len_ref[0]
+
+    def live_of(base, rows):
+        return ((lax.broadcasted_iota(jnp.int32, (rows, 128), 0) + base) < length).astype(f32)
+
+    @pl.when(i == 0)
+    def _():
+        gain = gain_ref[...]
+
+        def norm(c, carry):
+            at = pl.ds(pl.multiple_of(c * 32, 32), 32)
+            v = x_ref[at, :].astype(f32)
+            centred = v - jnp.mean(v, axis=1, keepdims=True)
+            inv = lax.rsqrt(jnp.mean(centred * centred, axis=1, keepdims=True) + EPS)
+            n = centred * inv
+            normed[at, :] = n
+            invs[at, :] = jnp.broadcast_to(inv, (32, 128))
+            scaled[at, :] = (n * gain).astype(bf)
+            return carry
+
+        lax.fori_loop(0, 16, norm, 0)
+        scaled_t[...] = scaled[...].T
+        cot_t[...] = ct_ref[...].T
+        for buf in (gat, dfl):
+            for h in range(2):
+                buf[h, pl.ds(0, 16), :] = jnp.zeros((16, 128), f32)
+                buf[h, pl.ds(528, 16), :] = jnp.zeros((16, 128), f32)
+        for s in range(8):
+            g_ref[s, pl.ds(1728, 64), :] = jnp.zeros((64, 128), bf)
+
+    dot = functools.partial(lax.dot_general, preferred_element_type=f32)
+    NN, NT = (((1,), (0,)), ((), ())), (((1,), (1,)), ((), ()))
+
+    def gate(c, carry):
+        base = pl.multiple_of(c * 128, 128)
+        at = pl.ds(base, 128)
+        live = live_of(base, 128)
+        v = dot(scaled[at, :], upv_ref[...], NN)
+        sg = jax.nn.sigmoid(dot(scaled[at, :], upg_ref[...], NN))
+        vals[at, :] = v
+        gsig[at, :] = sg
+        dact[at, :] = dot(ct_ref[at, :], dt_ref[...], NN)
+        for h in range(2):
+            cols = slice(h * 128, h * 128 + 128)
+            gat[h, pl.ds(base + 16, 128), :] = (v[:, cols] * sg[:, cols] * live).astype(bf).astype(f32)
+        return carry
+
+    lax.fori_loop(0, 4, gate, 0)
+    R = 64
+    for h in range(2):
+        cols = pl.ds(h * 128, 128)
+        kacc[...] = jnp.zeros_like(kacc)
+
+        def forward(c, carry):
+            base = pl.multiple_of(c * R, R)
+            at = pl.ds(base, R)
+            live = live_of(base, R)
+            total = jnp.zeros((R, 128), f32)
+            for r in range(8):
+                window = gat[h, pl.ds(base + r, R + 24), :]
+                for j in range(4):
+                    total = total + taps_ref[pl.ds(r + 8 * j, 1), cols] * window[8 * j : 8 * j + R]
+            sg = jax.nn.sigmoid(total)
+            act[at, cols] = (total * sg * live).astype(bf)
+            d = dact[at, cols] * live * sg * (1.0 + total * (1.0 - sg))
+            dfl[h, pl.ds(base + 16, R), :] = d
+            for r in range(8):
+                window = gat[h, pl.ds(base + r, R + 24), :]
+                for j in range(4):
+                    prod = d * window[8 * j : 8 * j + R]
+                    k = r + 8 * j
+                    kacc[k] = kacc[k] + jnp.sum(prod.reshape(R // 8, 8, 128), axis=0)
+            return carry
+
+        lax.fori_loop(0, 512 // R, forward, 0)
+        kall[i * 2 + h] = jnp.sum(kacc[...], axis=1)
+
+        def backward(c, carry):
+            base = pl.multiple_of(c * R, R)
+            at = pl.ds(base, R)
+            live = live_of(base, R)
+            total = jnp.zeros((R, 128), f32)
+            for r in range(8):
+                first = r if r else 8
+                window = dfl[h, pl.ds(base + first, R + 24), :]
+                for j in range(4):
+                    total = total + taps_ref[pl.ds(32 - first - 8 * j, 1), cols] * window[8 * j : 8 * j + R]
+            total = total * live
+            sg, v = gsig[at, cols], vals[at, cols]
+            dpv[at, cols] = (total * sg).astype(bf)
+            dpg[at, cols] = (total * v * sg * (1.0 - sg)).astype(bf)
+            return carry
+
+        lax.fori_loop(0, 512 // R, backward, 0)
+
+    def pack(part, start, tiles_wide, column):
+        for h in range(2):
+            for s in range(8):
+                for rt in range(6):
+                    at = start + (rt * tiles_wide + column + h) * 16
+                    row = s * 96 + rt * 16
+                    g_ref[s, pl.ds(pl.multiple_of(at, 16), 16), :] = part[row : row + 16, h * 128 : h * 128 + 128]
+
+    pack(dot(cot_t[...], act[...], NN).astype(bf), 1152, 6, i * 2)
+    pack(dot(scaled_t[...], dpv[...], NN).astype(bf), 0, 12, i * 2)
+    pack(dot(scaled_t[...], dpg[...], NN).astype(bf), 0, 12, 6 + i * 2)
+    m = dot(act[...], dt_ref[...], NT)
+    d = dot(dpv[...], upv_ref[...], NT) + dot(dpg[...], upg_ref[...], NT)
+
+    @pl.when(i == 0)
+    def _():
+        mixed[...] = m
+        dsc[...] = d
+
+    @pl.when(i > 0)
+    def _():
+        mixed[...] += m
+        dsc[...] += d
+
+    @pl.when(i == 2)
+    def _():
+        gain = gain_ref[...]
+
+        def finish(c, gsum):
+            at = pl.ds(pl.multiple_of(c * 32, 32), 32)
+            res_ref[at, :] = (x_ref[at, :].astype(f32) + mixed[at, :]).astype(bf)
+            ds, n = dsc[at, :], normed[at, :]
+            prod = ds * n
+            dn = ds * gain
+            inv = invs[at, :][:, :1]
+            grad = inv * (dn - jnp.mean(dn, axis=1, keepdims=True)
+                          - n * jnp.mean(prod * gain, axis=1, keepdims=True))
+            gin_ref[at, :] = (ct_ref[at, :].astype(f32) + grad).astype(bf)
+            return gsum + jnp.sum(prod.reshape(4, 8, 768), axis=0)
+
+        gsum = lax.fori_loop(0, 16, finish, jnp.zeros((8, 768), f32))
+        gsum = jnp.sum(gsum, axis=0, keepdims=True)
+        small = jnp.concatenate([kall[b] for b in range(6)], axis=1)
+        small = jnp.concatenate([small, jnp.broadcast_to(gsum, (16, 768))], axis=0)
+        for s in range(8):
+            g_ref[s, pl.ds(1728, 48), pl.ds(0, 96)] = small[:, s * 96 : s * 96 + 96].astype(bf)
+
+
+def layer(lengths, frames, cot, full, taps, gain):
+    f32, bf = jnp.float32, jnp.bfloat16
+    whole = lambda r, c: pl.BlockSpec((r, c), lambda i: (0, 0))
+    return pl.pallas_call(
+        layer_kernel,
+        grid=(3,),
+        out_shape=(
+            jax.ShapeDtypeStruct((512, 768), bf),
+            jax.ShapeDtypeStruct((512, 768), bf),
+            jax.ShapeDtypeStruct((8, 1792, 128), bf),
+        ),
+        in_specs=[
+            pl.BlockSpec(memory_space=pltpu.SMEM),
+            whole(512, 768),
+            whole(512, 768),
+            pl.BlockSpec((768, 256), lambda i: (0, i)),
+            pl.BlockSpec((768, 256), lambda i: (0, 3 + i)),
+            pl.BlockSpec((768, 256), lambda i: (0, 6 + i)),
+            pl.BlockSpec((32, 256), lambda i: (0, i)),
+            whole(1, 768),
+        ],
+        out_specs=(
+            whole(512, 768),
+            whole(512, 768),
+            pl.BlockSpec((8, 1792, 128), lambda i: (0, 0, 0)),
+        ),
+        scratch_shapes=[
+            pltpu.VMEM((512, 768), f32),
+            pltpu.VMEM((512, 128), f32),
+            pltpu.VMEM((512, 768), bf),
+            pltpu.VMEM((768, 512), bf),
+            pltpu.VMEM((768, 512), bf),
+            pltpu.VMEM((512, 256), f32),
+            pltpu.VMEM((512, 256), f32),
+            pltpu.VMEM((512, 256), f32),
+            pltpu.VMEM((2, 544, 128), f32),
+            pltpu.VMEM((2, 544, 128), f32),
+            pltpu.VMEM((512, 256), bf),
+            pltpu.VMEM((512, 256), bf),
+            pltpu.VMEM((512, 256), bf),
+            pltpu.VMEM((512, 768), f32),
+            pltpu.VMEM((512, 768), f32),
+            pltpu.VMEM((32, 8, 128), f32),
+            pltpu.VMEM((6, 32, 128), f32),
+        ],
+        compiler_params=pltpu.CompilerParams(vmem_limit_bytes=48 * 1024 * 1024),
+        name="layer",
+    )(lengths, frames, cot, full, full, full, taps, gain)
+
+
+def body(frames_in, lengths, up_weight, norm_gain, conv_kernel, down_weight, cotangent):
+    bf = jnp.bfloat16
+    small = jnp.pad(jnp.concatenate([conv_kernel, norm_gain[None, :]], axis=0), ((0, 63), (0, 32)))
+    packed = jnp.concatenate([up_weight, down_weight.T, small], axis=1)
+    full = gather_weights(packed)
+    small = full[:, 2304:].reshape(8, 96, 128)[:, :33, :96].transpose(1, 0, 2).reshape(33, 768)
+    small = small.astype(jnp.float32)
+    result, grad_in, parts = layer(
+        lengths, frames_in.reshape(512, 768), cotangent.reshape(512, 768), full, small[:32], small[32:]
     )
-
-
-def body(frames_in, lengths, up_weight, norm_gain, conv_kernel, down_weight, cotangent):
-    utts, frames, width = frames_in.shape
-    chans = up_weight.shape[1] // 2
-    count_taps = conv_kernel.shape[0]
-    front = count_taps // 2
-    back = count_taps - 1 - front
-    row_count = utts * frames
-    bf = jnp.bfloat16
-    packed = jnp.concatenate(
-        [up_weight, down_weight.T, conv_kernel.T, norm_gain[:, None], jnp.zeros((96, 95), bf)], axis=1
-    )
-    full = gather_weights(packed)
-    up_full = full[:, :1536]
-    down_t = full[:, 1536:2304]
-    small = full[:, 2304:].T
-    taps_bf, gain_bf = small[:32], small[32]
-
-    live = (jnp.arange(frames, dtype=jnp.int32)[None, :] < lengths[:, None]).astype(jnp.float32)
-    live_col = live.reshape(row_count, 1)
-    inputs = frames_in.reshape(row_count, width).astype(jnp.float32)
-    normed, inv_std = normalize(inputs)
-    gain_f = gain_bf.astype(jnp.float32)
-    scaled = (normed * gain_f).astype(bf)
-    projected = jnp.dot(scaled, up_full, preferred_element_type=jnp.float32)
-    values_half = projected[:, :chans]
-    gate_sig = jax.nn.sigmoid(projected[:, chans:])
-    gated = (values_half * gate_sig * live_col).astype(bf)
-    taps_f = taps_bf.astype(jnp.float32)
-    gated_f = gated.astype(jnp.float32).reshape(utts, frames, chans)
-    filtered = depthwise(gated_f, taps_f, front, back).reshape(row_count, chans)
-    activated = (jax.nn.silu(filtered) * live_col).astype(bf)
-    upstream = cotangent.reshape(row_count, width)
-    mixed = lax.dot_general(
-        activated, down_t, (((1,), (1,)), ((), ())), preferred_element_type=jnp.float32
-    )
-    d_act = jnp.dot(upstream, down_t, preferred_element_type=jnp.float32)
-    result = (inputs + mixed).astype(bf)
-    down_part = lax.dot_general(
-        upstream, activated, (((0,), (0,)), ((), ())), preferred_element_type=jnp.float32
-    )
-    factor = 1.0 / float(utts * 512 * frames) ** 0.5
-    filt_sig = jax.nn.sigmoid(filtered)
-    d_filt = d_act * live_col * filt_sig * (1.0 + filtered * (1.0 - filt_sig))
-    d_filt3 = d_filt.reshape(utts, frames, chans)
-    kernel_part = tap_grads(d_filt3, gated_f, front, back)
-    d_gated = depthwise(d_filt3, taps_f[::-1], back, front).reshape(row_count, chans) * live_col
-    d_proj = jnp.concatenate(
-        [d_gated * gate_sig, d_gated * values_half * gate_sig * (1.0 - gate_sig)], axis=1
-    ).astype(bf)
-    up_part = lax.dot_general(
-        scaled, d_proj, (((0,), (0,)), ((), ())), preferred_element_type=jnp.float32
-    )
-    d_scaled = lax.dot_general(
-        d_proj, up_full, (((1,), (1,)), ((), ())), preferred_element_type=jnp.float32
-    )
-    gain_part = jnp.sum(d_scaled * normed, axis=0)
-    d_normed = d_scaled * gain_f
-    d_inputs = inv_std * (
-        d_normed
-        - jnp.mean(d_normed, axis=1, keepdims=True)
-        - normed * jnp.mean(d_normed * normed, axis=1, keepdims=True)
-    )
-    grad_in = (upstream.astype(jnp.float32) + d_inputs).astype(bf)
-
-    taps_tiles = jnp.pad(
-        kernel_part.astype(bf).reshape(32, 8, 96).transpose(1, 0, 2), ((0, 0), (0, 0), (0, 32))
-    ).reshape(8, 4, 8, 128)
-    gain_tiles = jnp.pad(
-        gain_part.astype(bf).reshape(8, 1, 1, 96), ((0, 0), (0, 3), (0, 7), (0, 32))
-    )
-    parts = jnp.concatenate(
-        [tiles(up_part.astype(bf), 12), tiles(down_part.astype(bf), 6), taps_tiles, gain_tiles], axis=1
-    ).reshape(4, 2, 2, 896, 128)
-    total = reduce_parts(parts, factor).reshape(224, 8, 128)
-    up_total = untiles(total[:144], 12)
-    down_total = untiles(total[144:216], 6).T
-    kernel_total = total[216:220].reshape(32, 128)[:, :96]
-    gain_total = total[220, 0, :96]
+    factor = 1.0 / 262144.0 ** 0.5
+    up_total, down_total, rest = reduce_parts(parts.reshape(4, 2, 2, 896, 128), factor)
     return (
-        result.reshape(utts, frames, width),
-        grad_in.reshape(utts, frames, width),
+        result.reshape(1, 512, 768),
+        grad_in.reshape(1, 512, 768),
         up_total,
-        gain_total,
-        kernel_total,
-        down_total,
+        rest[32, :96],
+        rest[:32, :96],
+        down_total.T,
     )
 
 

time: 161 us -> 140 us (0.87)
  Pallas kernels: 95.2 us -> 126 us
  other arithmetic: 27.6 us -> 2.58 us
  local copies, waits for them, and re-layouts: 22.8 us -> 9.06 us
  matrix products: 13.4 us -> 0 us
    pallas_call x1 -> x2, Pallas kernels: 68.4 us -> 99 us  [the longest x1 68.3 us: reduce_parts(): pl.pallas_call(lambda *refs: reduce_kernel(factor, *refs), out_shape=(jax...]
    dot_general x6 -> x0, matrix products: 13.4 us -> none  [the longest x1 5.68 us: body(): d_act = jnp.dot(upstream, down_t, preferred_element_type=jnp.float32)]
    another operation x2 -> x0, other arithmetic: 9.67 us -> none
    slice x4 -> x7, local copies, waits for them, and re-layouts: 10.2 us -> 2.46 us  [the longest x1 1.32 us: body(): rest[:32, :96]]
    reduce_sum x4 -> x0, other arithmetic: 7.14 us -> none  [the longest x2 4.34 us: tap_grads(): jnp.sum(grad * padded[:, offset:offset + frames], axis=(0, 1))]
    add x1 -> x0, other arithmetic: 6.66 us -> none  [depthwise(): total = total + taps_f[offset] * padded[:, offset:offset + frames]]
    another operation x33 -> x0, local copies, waits for them, and re-layouts: 2.76 us -> none  [tap_grads(): jnp.stack([jnp.sum(grad * padded[:, offset:offset + frames], axis=(0, 1))...]
    reshape x2 -> x0, other arithmetic: 1.96 us -> none  [the longest x1 1.52 us: body(): grad_in.reshape(utts, frames, width)]
where the time goes in v2:
time: 140 us; the launch traced here: 139 us
  Pallas kernels  126 us (90%)
  local copies, waits for them, and re-layouts  9.06 us (6%)
  other arithmetic  2.58 us (2%)
  between operations  1.48 us (1%)
    pallas_call x1, Pallas kernels, reduce_parts(): pl.pallas_call(lambda *refs: reduce_kernel(factor, *refs), out_shape=(jax...  68.3 us
    pallas_call x1, Pallas kernels, layer(): pl.pallas_call(layer_kernel, grid=(3,), out_shape=(jax.ShapeDtypeStruct((...  30.7 us
    pallas_call x1, Pallas kernels, gather_weights(): pl.pallas_call(gather_kernel, out_shape=jax.ShapeDtypeStruct((768, WIDE),...  26.7 us
    unnamed x8, local copies, waits for them, and re-layouts  5.41 us

profile of v2, /device:TPU:1, one launch (start us, length us, event | category | flops | bytes accessed | tf_op | source)
XLA Modules:
  0.0 138.9 jit_solution(159744784840170961)
XLA Ops:
  0.6 0.0 copy-start.2
  0.6 0.0 copy-start.1
  1.4 0.7 fusion.5
  2.1 1.8 %pad_maximum_fusion.w_ref = bf16[96,2432]{1,0:T(8,128)(2,1)} fusion(bf16[96,128]{1,0:T(8,128)(2,1)S(1)} %fusion.5, bf16[96,768]{1,0:T(8,128)(2,1)} %bitcast.18, bf16[96,1536]{1,0:T(8,128)(2,1)} %param.9), kind=kLoop, calls=%fused_computation | loop fusion | flops 1400832 | bytes 933888 | tf_op jit(solution)/shard_map/concatenate | solution.py:569
  4.0 26.7 %gather_weights.1.upv_ref.upg_ref.dt_ref = bf16[768,2432]{1,0:T(8,128)(2,1)} custom-call(bf16[96,2432]{1,0:T(8,128)(2,1)} %pad_maximum_fusion.w_ref), custom_call_target="tpu_custom_call" | custom-call | tf_op jit(solution)/shard_map/gather_weights/pallas_call | solution.py:122
  30.7 0.9 slice.24
  31.8 0.1 slice.27.taps_ref
  31.9 0.1 slice.29.gain_ref
  31.9 0.0 copy-done.2
  31.9 0.0 copy-done.1
  31.9 30.7 %layer.1 = (bf16[512,768]{1,0:T(8,128)(2,1)}, bf16[512,768]{1,0:T(8,128)(2,1)}, bf16[8,1792,128]{2,1,0:T(8,128)(2,1)S(1)}) custom-call(s32[1]{0:T(128)S(6)} %copy.18.len_ref, bf16[512,768]{1,0:T(8,128)(2,1)S(1)} %bitcast.14, bf16[512,768]{1,0:T(8,128)(2,1)S(1)} %bitcast.15, bf16[768,2432]{1,0:T(8,128)(2,1)} %gather_weights.1.upv_ref.upg_ref.dt_ref, ...), custom_call_target="tpu_custom_call" | custom-call | tf_op jit(solution)/shard_map/layer/pallas_call | solution.py:519
  62.7 0.0 copy-start
  62.7 1.8 %copy-done = bf16[8,1792,128]{2,1,0:T(8,128)(2,1)} copy-done((bf16[8,1792,128]{2,1,0:T(8,128)(2,1)}, bf16[8,1792,128]{2,1,0:T(8,128)(2,1)S(1)}, u32[]{:S(2)}) %copy-start) | copy-done | bytes 3670040
  64.4 68.3 %reduce_parts.1 = (f32[96,1536]{1,0:T(8,128)}, f32[96,768]{1,0:T(8,128)}, f32[48,128]{1,0:T(8,128)}) custom-call(bf16[4,2,2,896,128]{4,3,2,1,0:T(8,128)(2,1)} %bitcast.13), custom_call_target="tpu_custom_call" | custom-call | tf_op jit(solution)/shard_map/reduce_parts/pallas_call | solution.py:335
  132.8 1.2 slice_bitcast_fusion
  133.9 1.3 slice.31
  135.3 1.9 %copy.19 = f32[96,1536]{1,0:T(8,128)} copy(f32[96,1536]{1,0:T(8,128)} %get-tuple-element.26) | data formatting | bytes 1179648
  137.2 1.7 %copy.20 = f32[768,96]{0,1:T(8,128)} copy(f32[768,96]{0,1:T(8,128)} %bitcast.17) | data formatting | bytes 589824
  (4 shorter events, 0.0 us)
Async XLA Ops:
  0.6 31.3 %copy-start.2 = (bf16[1,512,768]{2,1,0:T(8,128)(2,1)S(1)}, bf16[1,512,768]{2,1,0:T(8,128)(2,1)}, u32[]{:S(2)}) copy-start(bf16[1,512,768]{2,1,0:T(8,128)(2,1)} %param.13) | copy-start | bytes 2359300
  0.6 31.3 %copy-start.1 = (bf16[1,512,768]{2,1,0:T(8,128)(2,1)S(1)}, bf16[1,512,768]{2,1,0:T(8,128)(2,1)}, u32[]{:S(2)}) copy-start(bf16[1,512,768]{2,1,0:T(8,128)(2,1)} %param.7) | copy-start | bytes 2359300
  62.7 1.8 %copy-start = (bf16[8,1792,128]{2,1,0:T(8,128)(2,1)}, bf16[8,1792,128]{2,1,0:T(8,128)(2,1)S(1)}, u32[]{:S(2)}) copy-start(bf16[8,1792,128]{2,1,0:T(8,128)(2,1)S(1)} %get-tuple-element.14) | copy-start | bytes 11010052

commit v3 on v1

v3 whole, which is shorter than its diff:
```python
import functools

import jax
import jax.numpy as jnp
from jax import lax
from jax.experimental import pallas as pl
from jax.experimental.pallas import tpu as pltpu
from jax.sharding import PartitionSpec as P

EPS = 1e-05
WIDE = 2432
CUT = 1280
MESH = pl.DeviceIdType.MESH


def place():
    rep, sh = lax.axis_index("replica"), lax.axis_index("shard")
    z, y_hi, core = rep // 4, (rep // 2) % 2, rep % 2
    x, y_lo = sh // 2, sh % 2
    return x, y_hi * 2 + y_lo, z, core


def device(x, y, z, core):
    return ((z * 2 + y // 2) * 2 + core, x * 2 + y % 2)


def greet(partners):
    barrier = pltpu.get_barrier_semaphore()
    for partner in partners:
        pl.semaphore_signal(barrier, inc=1, device_id=partner, device_id_type=MESH)
    pl.semaphore_wait(barrier, len(partners))


def gather_kernel(w_ref, out_ref, local_sem, send_sem, recv_sem):
    x, y, z, core = place()
    y_lo = y % 2
    xp, xm, x2 = (x + 1) % 4, (x + 3) % 4, (x + 2) % 4
    yp, ym = (y + 1) % 4, (y + 3) % 4
    to_xp, to_xm = device(xp, y, z, core), device(xm, y, z, core)
    to_yp, to_ym = device(x, yp, z, core), device(x, ym, z, core)
    to_sib = device(x, y, z, 1 - core)
    greet([to_xp, to_xm, to_yp, to_ym, to_sib])

    def rows(bx, byl):
        return pl.ds(pl.multiple_of((bx * 2 + byl) * 96 + core * 48, 16), 48)

    LO, HI, ALL = pl.ds(0, CUT), pl.ds(CUT, WIDE - CUT), pl.ds(0, WIDE)
    own = pl.multiple_of((x * 2 + y_lo) * 96, 16)
    local = pltpu.make_async_copy(w_ref, out_ref.at[pl.ds(own, 96)], local_sem)
    local.start()
    mine = pl.ds(pl.multiple_of(core * 48, 16), 48)
    sent = []

    def send(index, bx, byl, cols, target, own_block=False):
        dst = out_ref.at[rows(bx, byl), cols]
        src = w_ref.at[mine, cols] if own_block else dst
        copy = pltpu.make_async_remote_copy(
            src_ref=src, dst_ref=dst, send_sem=send_sem.at[index], recv_sem=recv_sem.at[index],
            device_id=target, device_id_type=MESH)
        copy.start()
        sent.append(copy)

    def arrive(index, bx, byl, cols):
        dst = out_ref.at[rows(bx, byl), cols]
        pltpu.make_async_remote_copy(
            src_ref=dst, dst_ref=dst, send_sem=send_sem.at[index], recv_sem=recv_sem.at[index],
            device_id=to_sib, device_id_type=MESH).wait_recv()

    oth = 1 - y_lo
    send(0, x, y_lo, ALL, to_xp, True)
    send(1, x, y_lo, ALL, to_xm, True)
    send(4, x, y_lo, LO, to_yp, True)
    send(8, x, y_lo, HI, to_ym, True)
    arrive(0, xm, y_lo, ALL)
    send(2, xm, y_lo, LO, to_xp)
    send(5, xm, y_lo, LO, to_yp)
    send(9, xm, y_lo, HI, to_ym)
    arrive(1, xp, y_lo, ALL)
    send(3, xp, y_lo, HI, to_xm)
    send(6, xp, y_lo, LO, to_yp)
    send(10, xp, y_lo, HI, to_ym)
    send(12, xm, y_lo, ALL, to_sib)
    send(13, xp, y_lo, ALL, to_sib)
    arrive(4, x, oth, LO)
    send(16, x, oth, LO, to_sib)
    arrive(8, x, oth, HI)
    send(20, x, oth, HI, to_sib)
    arrive(2, x2, y_lo, LO)
    send(7, x2, y_lo, LO, to_yp)
    send(14, x2, y_lo, LO, to_sib)
    arrive(3, x2, y_lo, HI)
    send(11, x2, y_lo, HI, to_ym)
    send(15, x2, y_lo, HI, to_sib)
    for k, bx in ((1, xm), (2, xp), (3, x2)):
        arrive(4 + k, bx, oth, LO)
        send(16 + k, bx, oth, LO, to_sib)
        arrive(8 + k, bx, oth, HI)
        send(20 + k, bx, oth, HI, to_sib)

    def sib_rows(bx, byl):
        return pl.ds(pl.multiple_of((bx * 2 + byl) * 96 + (1 - core) * 48, 16), 48)

    def arrive_sib(index, bx, byl, cols):
        dst = out_ref.at[sib_rows(bx, byl), cols]
        pltpu.make_async_remote_copy(
            src_ref=dst, dst_ref=dst, send_sem=send_sem.at[index], recv_sem=recv_sem.at[index],
            device_id=to_sib, device_id_type=MESH).wait_recv()

    arrive_sib(12, xm, y_lo, ALL)
    arrive_sib(13, xp, y_lo, ALL)
    arrive_sib(14, x2, y_lo, LO)
    arrive_sib(15, x2, y_lo, HI)
    for k, bx in ((0, x), (1, xm), (2, xp), (3, x2)):
        arrive_sib(16 + k, bx, oth, LO)
        arrive_sib(20 + k, bx, oth, HI)
    for copy in sent:
        copy.wait_send()
    local.wait()


def gather_weights(packed):
    return pl.pallas_call(
        gather_kernel,
        out_shape=jax.ShapeDtypeStruct((768, WIDE), jnp.bfloat16),
        in_specs=[pl.BlockSpec(memory_space=pltpu.VMEM)],
        out_specs=pl.BlockSpec(memory_space=pltpu.VMEM),
        scratch_shapes=[
            pltpu.SemaphoreType.DMA,
            pltpu.SemaphoreType.DMA((24,)),
            pltpu.SemaphoreType.DMA((24,)),
        ],
        compiler_params=pltpu.CompilerParams(collective_id=0, has_side_effects=True),
        name="gather_weights",
    )(packed)


def add_rows(rows, step, dst, terms):
    def one(i, carry):
        at = pl.ds(pl.multiple_of(i * step, 16), step)
        total = terms[0](at).astype(jnp.float32)
        for term in terms[1:]:
            total = total + term(at).astype(jnp.float32)
        dst(at, total)
        return carry

    lax.fori_loop(0, rows // step, one, 0)


ROWS, START = (288, 288, 320), (0, 288, 576)


def layer_kernel(factor, len_ref, x_ref, ct_ref, w_ref, taps_ref, gain_ref,
                 res_ref, gin_ref, up_ref, down_ref, rest_ref,
                 normed, invs, scaled, scaled_t, cot_t, vals, gsig, dact, gat, dfl, act, dpv, dpg,
                 mixed, dsc, kacc, kall,
                 g, cr, cs, xr, xq, xs, yr, yq, zs, zr, fin,
                 send_sem, recv_sem, zsend, zrecv, asend, arecv):
    f32, bf = jnp.float32, jnp.bfloat16
    length = len_ref[0]
    x, y, z, core = place()
    y_lo, y_hi = y % 2, y // 2
    xp, xm, x2 = (x + 1) % 4, (x + 3) % 4, (x + 2) % 4
    yp, ym, y2 = (y + 1) % 4, (y + 3) % 4, (y + 2) % 4
    to_xp, to_xm = device(xp, y, z, core), device(xm, y, z, core)
    to_yp, to_ym = device(x, yp, z, core), device(x, ym, z, core)
    to_y2 = device(x, y2, z, core)
    to_sib = device(x, y, z, 1 - core)

    barrier = pltpu.get_barrier_semaphore()
    for partner in (to_xp, to_xm, to_yp, to_ym, to_y2, to_sib):
        pl.semaphore_signal(barrier, inc=1, device_id=partner, device_id_type=MESH)

    def hello(d, carry):
        pl.semaphore_signal(barrier, inc=1, device_id=device(x, y, (z + d) % 16, core), device_id_type=MESH)
        return carry

    lax.fori_loop(1, 16, hello, 0)
    sent = []

    def copy(index, src, dst, target):
        return pltpu.make_async_remote_copy(
            src_ref=src, dst_ref=dst, send_sem=send_sem.at[index], recv_sem=recv_sem.at[index],
            device_id=target, device_id_type=MESH)

    def send(index, src, dst, target):
        c = copy(index, src, dst, target)
        c.start()
        sent.append(c)

    def arrive(index, dst):
        copy(index, dst, dst, to_sib).wait_recv()


    def live_of(base, rows):
        return ((lax.broadcasted_iota(jnp.int32, (rows, 128), 0) + base) < length).astype(f32)


    gain = gain_ref[...]

    def norm(c, carry):
        at = pl.ds(pl.multiple_of(c * 32, 32), 32)
        v = x_ref[at, :].astype(f32)
        centred = v - jnp.mean(v, axis=1, keepdims=True)
        inv = lax.rsqrt(jnp.mean(centred * centred, axis=1, keepdims=True) + EPS)
        n = centred * inv
        normed[at, :] = n
        invs[at, :] = jnp.broadcast_to(inv, (32, 128))
        scaled[at, :] = (n * gain).astype(bf)
        return carry

    lax.fori_loop(0, 16, norm, 0)
    scaled_t[...] = scaled[...].T
    cot_t[...] = ct_ref[...].T
    for buf in (gat, dfl):
        for h in range(2):
            buf[h, pl.ds(0, 16), :] = jnp.zeros((16, 128), f32)
            buf[h, pl.ds(528, 16), :] = jnp.zeros((16, 128), f32)
    for s in range(8):
        g[2, s // 2, s % 2, 1, pl.ds(256, 64), :] = jnp.zeros((64, 128), bf)


    dot = functools.partial(lax.dot_general, preferred_element_type=f32)
    NN, NT = (((1,), (0,)), ((), ())), (((1,), (1,)), ((), ()))


    order = (x2, xp, xm, x)

    def core_start(b):
        n = pl.ds(0, ROWS[b])
        for k, bx in enumerate(order):
            send(b * 10 + k, g.at[b, bx, :, 1 - core, n], cr.at[b, bx, :, n], to_sib)

    def core_sum(b, k):
        bx, n = order[k], ROWS[b]
        arrive(b * 10 + k, cr.at[b, bx, :, pl.ds(0, n)])
        for j in range(2):
            def put(at, v):
                cs[b, bx, j, at, :] = v.astype(bf)
            add_rows(n, n // 4 if n == 320 else n // 3, put,
                     [lambda at: g[b, bx, j, core, at, :], lambda at: cr[b, bx, j, at, :]])

    def x_first(b):
        n, at = b * 10, pl.ds(0, ROWS[b])
        core_sum(b, 0)
        send(n + 4, cs.at[b, x2, 0, at], xq.at[b, 0, at], to_xp)
        send(n + 5, cs.at[b, x2, 1, at], xq.at[b, 1, at], to_xm)
        core_sum(b, 1)
        send(n + 6, cs.at[b, xp, 1, at], xr.at[b, 0, 1, at], to_xp)
        core_sum(b, 2)
        send(n + 7, cs.at[b, xm, 0, at], xr.at[b, 1, 0, at], to_xm)
        core_sum(b, 3)

    def x_second(b):
        n, rows = b * 10, pl.ds(0, ROWS[b])
        step = ROWS[b] // 4 if ROWS[b] == 320 else ROWS[b] // 3
        for q, bx, target in ((0, xp, to_xp), (1, xm, to_xm)):
            arrive(n + 4 + q, xq.at[b, q, rows])

            def put(at, v):
                cs[b, bx, q, at, :] = v.astype(bf)

            add_rows(ROWS[b], step, put, [lambda at: cs[b, bx, q, at, :], lambda at: xq[b, q, at, :]])
            send(n + 8 + q, cs.at[b, bx, q, rows], xr.at[b, q, q, rows], target)

    def x_last(b):
        n, rows = b * 10, pl.ds(0, ROWS[b])
        step = ROWS[b] // 4 if ROWS[b] == 320 else ROWS[b] // 3
        arrive(n + 6, xr.at[b, 0, 1, rows])
        arrive(n + 7, xr.at[b, 1, 0, rows])
        arrive(n + 8, xr.at[b, 0, 0, rows])
        arrive(n + 9, xr.at[b, 1, 1, rows])
        for j in range(2):
            def put(at, v):
                xs[j, pl.ds(pl.multiple_of(START[b] + at.start, 16), step), :] = v.astype(bf)
            add_rows(ROWS[b], step, put, [lambda at: cs[b, x, j, at, :], lambda at: xr[b, 0, j, at, :],
                                          lambda at: xr[b, 1, j, at, :]])

    def pack(b, part, kind):
        for h in range(2):
            for s in range(8):
                for rt in range(6):
                    t = kind * 12 + rt * 2 + h
                    per, row = ROWS[b] // 16, s * 96 + rt * 16
                    g[b, s // 2, s % 2, t // per, pl.ds(t % per * 16, 16), :] = part[
                        row : row + 16, h * 128 : h * 128 + 128]

    R = 64
    for b in range(3):
        v_cols, g_cols, d_cols = pl.ds(b * 256, 256), pl.ds(768 + b * 256, 256), pl.ds(1536 + b * 256, 256)
        def gate(c, carry):
            base = pl.multiple_of(c * 128, 128)
            at = pl.ds(base, 128)
            live = live_of(base, 128)
            v = dot(scaled[at, :], w_ref[:, v_cols], NN)
            sg = jax.nn.sigmoid(dot(scaled[at, :], w_ref[:, g_cols], NN))
            vals[at, :] = v
            gsig[at, :] = sg
            dact[at, :] = dot(ct_ref[at, :], w_ref[:, d_cols], NN)
            for h in range(2):
                cols = slice(h * 128, h * 128 + 128)
                gat[h, pl.ds(base + 16, 128), :] = (v[:, cols] * sg[:, cols] * live).astype(bf).astype(f32)
            return carry

        lax.fori_loop(0, 4, gate, 0)

        for h in range(2):
            cols = pl.ds(h * 128, 128)
            taps_cols = pl.ds(b * 256 + h * 128, 128)
            kacc[...] = jnp.zeros_like(kacc)

            def forward(c, carry):
                base = pl.multiple_of(c * R, R)
                at = pl.ds(base, R)
                live = live_of(base, R)
                total = jnp.zeros((R, 128), f32)
                for r in range(8):
                    window = gat[h, pl.ds(base + r, R + 24), :]
                    for j in range(4):
                        total = total + taps_ref[pl.ds(r + 8 * j, 1), taps_cols] * window[8 * j : 8 * j + R]
                sg = jax.nn.sigmoid(total)
                act[at, cols] = (total * sg * live).astype(bf)
                d = dact[at, cols] * live * sg * (1.0 + total * (1.0 - sg))
                dfl[h, pl.ds(base + 16, R), :] = d
                for r in range(8):
                    window = gat[h, pl.ds(base + r, R + 24), :]
                    for j in range(4):
                        prod = d * window[8 * j : 8 * j + R]
                        k = r + 8 * j
                        kacc[k] = kacc[k] + jnp.sum(prod.reshape(R // 8, 8, 128), axis=0)
                return carry

            lax.fori_loop(0, 512 // R, forward, 0)
            kall[b * 2 + h] = jnp.sum(kacc[...], axis=1)

            def backward(c, carry):
                base = pl.multiple_of(c * R, R)
                at = pl.ds(base, R)
                live = live_of(base, R)
                total = jnp.zeros((R, 128), f32)
                for r in range(8):
                    first = r if r else 8
                    window = dfl[h, pl.ds(base + first, R + 24), :]
                    for j in range(4):
                        total = total + taps_ref[pl.ds(32 - first - 8 * j, 1), taps_cols] * window[8 * j : 8 * j + R]
                total = total * live
                sg, v = gsig[at, cols], vals[at, cols]
                dpv[at, cols] = (total * sg).astype(bf)
                dpg[at, cols] = (total * v * sg * (1.0 - sg)).astype(bf)
                return carry

            lax.fori_loop(0, 512 // R, backward, 0)


            if b and not h:
                x_first(b - 1)
                if b == 2:
                    x_last(0)
        if b:
            x_second(b - 1)
        pack(b, dot(scaled_t[...], dpv[...], NN).astype(bf), 0)
        pack(b, dot(scaled_t[...], dpg[...], NN).astype(bf), 1)
        pack(b, dot(cot_t[...], act[...], NN).astype(bf), 2)
        if b == 0:
            pl.semaphore_wait(barrier, 21)
        if b < 2:
            core_start(b)
        m = dot(act[...], w_ref[:, d_cols], NT)
        d = dot(dpv[...], w_ref[:, v_cols], NT) + dot(dpg[...], w_ref[:, g_cols], NT)
        if b:
            mixed[...] += m
            dsc[...] += d
        else:
            mixed[...] = m
            dsc[...] = d

    def finish(c, gsum):
        at = pl.ds(pl.multiple_of(c * 32, 32), 32)
        ds, n = dsc[at, :], normed[at, :]
        prod = ds * n
        dn = ds * gain
        inv = invs[at, :][:, :1]
        grad = inv * (dn - jnp.mean(dn, axis=1, keepdims=True)
                      - n * jnp.mean(prod * gain, axis=1, keepdims=True))
        gin_ref[at, :] = (ct_ref[at, :].astype(f32) + grad).astype(bf)
        return gsum + jnp.sum(prod.reshape(4, 8, 768), axis=0)

    gsum = lax.fori_loop(0, 16, finish, jnp.zeros((8, 768), f32))
    gsum = jnp.sum(gsum, axis=0, keepdims=True)
    small = jnp.concatenate([kall[b] for b in range(6)], axis=1)
    small = jnp.concatenate([small, jnp.broadcast_to(gsum, (16, 768))], axis=0)
    for s in range(8):
        g[2, s // 2, s % 2, 1, pl.ds(256, 48), pl.ds(0, 96)] = small[:, s * 96 : s * 96 + 96].astype(bf)
    core_start(2)
    x_last(1)
    x_first(2)
    x_second(2)
    x_last(2)
    def part(yy, half, rows=224):
        return xs.at[yy % 2, pl.ds(pl.multiple_of((yy // 2) * 448 + half * 224, 16), rows)]

    send(30, part(y2, 0), yq.at[0], to_yp)
    send(31, part(y2, 1), yq.at[1], to_ym)
    send(32, part(yp, 1), yr.at[0, 1], to_yp)
    send(33, part(ym, 0), yr.at[1, 0], to_ym)
    arrive(30, yq.at[0])
    dst_p = part(yp, 0)

    def put_yp(at, v):
        dst_p[at, :] = v.astype(jnp.bfloat16)

    add_rows(224, 32, put_yp, [lambda at: dst_p[at, :], lambda at: yq[0, at, :]])
    send(34, part(yp, 0), yr.at[0, 0], to_yp)
    arrive(31, yq.at[1])
    dst_m = part(ym, 1)

    def put_ym(at, v):
        dst_m[at, :] = v.astype(jnp.bfloat16)

    add_rows(224, 32, put_ym, [lambda at: dst_m[at, :], lambda at: yq[1, at, :]])
    send(35, part(ym, 1), yr.at[1, 1], to_ym)
    arrive(32, yr.at[0, 1])
    arrive(33, yr.at[1, 0])
    arrive(34, yr.at[0, 0])
    arrive(35, yr.at[1, 1])
    zs[pl.ds(448, 64), :] = jnp.zeros((64, 128), jnp.bfloat16)
    for half in range(2):
        mine = part(y, half)

        def put(at, v):
            zs[pl.ds(pl.multiple_of(half * 224 + at.start, 16), 32), :] = v.astype(jnp.bfloat16)

        add_rows(224, 32, put, [lambda at: mine[at, :], lambda at: yr[0, half, at, :], lambda at: yr[1, half, at, :]])


    def piece(p):
        return pl.ds(pl.multiple_of(p * 32, 32), 32)

    def z_copy(d):
        to = (z + d) % 16
        return pltpu.make_async_remote_copy(
            src_ref=zs.at[piece(to)], dst_ref=zr.at[d], send_sem=zsend.at[d], recv_sem=zrecv.at[d],
            device_id=device(x, y, to, core), device_id_type=MESH)

    def z_start(d, carry):
        z_copy(d).start()
        return carry

    lax.fori_loop(1, 16, z_start, 0)

    def residual(c, carry):
        at = pl.ds(pl.multiple_of(c * 64, 64), 64)
        res_ref[at, :] = (x_ref[at, :].astype(f32) + mixed[at, :]).astype(bf)
        return carry

    lax.fori_loop(0, 8, residual, 0)

    def z_add(d, total):
        z_copy(d).wait_recv()
        return total + zr[d].astype(jnp.float32)

    total = lax.fori_loop(1, 16, z_add, zs[piece(z), :].astype(jnp.float32))
    mine_at = fin.at[core, y_hi]
    mine_at[piece(z), :] = total.astype(jnp.bfloat16)

    def a_copy(d, p):
        at = fin.at[core, y_hi, piece(p)]
        return pltpu.make_async_remote_copy(
            src_ref=at, dst_ref=at, send_sem=asend.at[d], recv_sem=arecv.at[d],
            device_id=device(x, y, (z + d) % 16, core), device_id_type=MESH)

    def a_start(d, carry):
        a_copy(d, z).start()
        return carry

    lax.fori_loop(1, 16, a_start, 0)

    def a_wait(d, carry):
        a_copy(d, (z + 16 - d) % 16).wait_recv()
        return carry

    lax.fori_loop(1, 16, a_wait, 0)
    both = fin.at[core, y_hi, pl.ds(0, 448)]
    send(36, both, both, to_y2)
    send(37, both, both, to_sib)
    far = fin.at[core, 1 - y_hi, pl.ds(0, 448)]
    arrive(36, far)
    send(38, far, far, to_sib)

    def z_done(d, carry):
        z_copy(d).wait_send()
        a_copy(d, z).wait_send()
        return carry

    lax.fori_loop(1, 16, z_done, 0)
    arrive(37, fin.at[1 - core, y_hi, pl.ds(0, 448)])
    arrive(38, fin.at[1 - core, 1 - y_hi, pl.ds(0, 448)])

    def tile(b, t):
        per = ROWS[b] // 16
        row = START[b] + t % per * 16
        return fin[t // per, row // 448, pl.ds(row % 448, 16), :].astype(f32) * factor

    for b in range(3):
        for h in range(2):
            at = (b * 2 + h) * 128
            for rt in range(6):
                rows = pl.ds(rt * 16, 16)
                up_ref[rows, pl.ds(at, 128)] = tile(b, rt * 2 + h)
                up_ref[rows, pl.ds(768 + at, 128)] = tile(b, 12 + rt * 2 + h)
                down_ref[rows, pl.ds(at, 128)] = tile(b, 24 + rt * 2 + h)
    for k in range(3):
        rest_ref[pl.ds(k * 16, 16), :] = tile(2, 36 + k)
    for c in sent:
        c.wait_send()


def layer(lengths, frames, cot, full, taps, gain, factor):
    f32, bf = jnp.float32, jnp.bfloat16
    vmem = pl.BlockSpec(memory_space=pltpu.VMEM)
    return pl.pallas_call(
        functools.partial(layer_kernel, factor),
        out_shape=(
            jax.ShapeDtypeStruct((512, 768), bf),
            jax.ShapeDtypeStruct((512, 768), bf),
            jax.ShapeDtypeStruct((96, 1536), f32),
            jax.ShapeDtypeStruct((96, 768), f32),
            jax.ShapeDtypeStruct((48, 128), f32),
        ),
        in_specs=[pl.BlockSpec(memory_space=pltpu.SMEM)] + [vmem] * 5,
        out_specs=(vmem,) * 5,
        scratch_shapes=[
            pltpu.VMEM((512, 768), f32),
            pltpu.VMEM((512, 128), f32),
            pltpu.VMEM((512, 768), bf),
            pltpu.VMEM((768, 512), bf),
            pltpu.VMEM((768, 512), bf),
            pltpu.VMEM((512, 256), f32),
            pltpu.VMEM((512, 256), f32),
            pltpu.VMEM((512, 256), f32),
            pltpu.VMEM((2, 544, 128), f32),
            pltpu.VMEM((2, 544, 128), f32),
            pltpu.VMEM((512, 256), bf),
            pltpu.VMEM((512, 256), bf),
            pltpu.VMEM((512, 256), bf),
            pltpu.VMEM((512, 768), f32),
            pltpu.VMEM((512, 768), f32),
            pltpu.VMEM((32, 8, 128), f32),
            pltpu.VMEM((6, 32, 128), f32),
            pltpu.VMEM((3, 4, 2, 2, 320, 128), bf),
            pltpu.VMEM((3, 4, 2, 320, 128), bf),
            pltpu.VMEM((3, 4, 2, 320, 128), bf),
            pltpu.VMEM((3, 2, 2, 320, 128), bf),
            pltpu.VMEM((3, 2, 320, 128), bf),
            pltpu.VMEM((2, 896, 128), bf),
            pltpu.VMEM((2, 2, 224, 128), bf),
            pltpu.VMEM((2, 224, 128), bf),
            pltpu.VMEM((512, 128), bf),
            pltpu.VMEM((16, 32, 128), bf),
            pltpu.VMEM((2, 2, 512, 128), bf),
            pltpu.SemaphoreType.DMA((39,)),
            pltpu.SemaphoreType.DMA((39,)),
            pltpu.SemaphoreType.DMA((16,)),
            pltpu.SemaphoreType.DMA((16,)),
            pltpu.SemaphoreType.DMA((16,)),
            pltpu.SemaphoreType.DMA((16,)),
        ],
        compiler_params=pltpu.CompilerParams(
            collective_id=1, has_side_effects=True, vmem_limit_bytes=48 * 1024 * 1024),
        name="layer",
    )(lengths, frames, cot, full, taps, gain)


def body(frames_in, lengths, up_weight, norm_gain, conv_kernel, down_weight, cotangent):
    bf = jnp.bfloat16
    small = jnp.pad(jnp.concatenate([conv_kernel, norm_gain[None, :]], axis=0), ((0, 63), (0, 32)))
    packed = jnp.concatenate([up_weight, down_weight.T, small], axis=1)
    full = gather_weights(packed)
    small = full[:, 2304:].reshape(8, 96, 128)[:, :33, :96].transpose(1, 0, 2).reshape(33, 768)
    small = small.astype(jnp.float32)
    factor = 1.0 / 262144.0 ** 0.5
    result, grad_in, up_total, down_total, rest = layer(
        lengths, frames_in.reshape(512, 768), cotangent.reshape(512, 768), full, small[:32], small[32:], factor
    )
    return (
        result.reshape(1, 512, 768),
        grad_in.reshape(1, 512, 768),
        up_total,
        rest[32, :96],
        rest[:32, :96],
        down_total.T,
    )


def solution(mesh):
    return jax.shard_map(
        body,
        mesh=mesh,
        in_specs=(
            P(("replica", "shard"), None, None),
            P(("replica", "shard")),
            P("shard", None),
            P("shard"),
            P(None, "shard"),
            P(None, "shard"),
            P(("replica", "shard"), None, None),
        ),
        out_specs=(
            P(("replica", "shard"), None, None),
            P(("replica", "shard"), None, None),
            P("shard", None),
            P("shard"),
            P(None, "shard"),
            P(None, "shard"),
        ),
        check_vma=False,
    )
```

time: 161 us -> 119 us (0.74)
  other arithmetic: 27.6 us -> 2.58 us
  local copies, waits for them, and re-layouts: 22.8 us -> 5.55 us
  Pallas kernels: 95.2 us -> 109 us
  matrix products: 13.4 us -> 0 us
    pallas_call x1, Pallas kernels: 68.4 us -> 82.2 us  [layer(): pl.pallas_call(functools.partial(layer_kernel, factor), out_shape=(jax.Sh...]
    dot_general x6 -> x0, matrix products: 13.4 us -> none  [the longest x1 5.68 us: body(): d_act = jnp.dot(upstream, down_t, preferred_element_type=jnp.float32)]
    another operation x2 -> x0, other arithmetic: 9.67 us -> none
    slice x4 -> x7, local copies, waits for them, and re-layouts: 10.2 us -> 1.74 us  [the longest x2 0.95 us: body(): full[:, 2304:].reshape(8, 96, 128)[:, :33, :96].transpose(1, 0, 2)]
    reduce_sum x4 -> x0, other arithmetic: 7.14 us -> none  [the longest x2 4.34 us: tap_grads(): jnp.sum(grad * padded[:, offset:offset + frames], axis=(0, 1))]
    add x1 -> x0, other arithmetic: 6.66 us -> none  [depthwise(): total = total + taps_f[offset] * padded[:, offset:offset + frames]]
    another operation x33 -> x0, local copies, waits for them, and re-layouts: 2.76 us -> none  [tap_grads(): jnp.stack([jnp.sum(grad * padded[:, offset:offset + frames], axis=(0, 1))...]
    reshape x2 -> x0, other arithmetic: 1.96 us -> none  [the longest x1 1.52 us: body(): grad_in.reshape(utts, frames, width)]
where the time goes in v3:
time: 119 us
  Pallas kernels  109 us (92%)
  local copies, waits for them, and re-layouts  5.55 us (5%)
  other arithmetic  2.58 us (2%)
  between operations  1.47 us (1%)
    pallas_call x1, Pallas kernels, layer(): pl.pallas_call(functools.partial(layer_kernel, factor), out_shape=(jax.Sh...  82.2 us
    pallas_call x1, Pallas kernels, gather_weights(): pl.pallas_call(gather_kernel, out_shape=jax.ShapeDtypeStruct((768, WIDE),...  26.8 us
    unnamed x8, local copies, waits for them, and re-layouts  3.29 us

profile of v3, /device:TPU:1, one launch (start us, length us, event | category | flops | bytes accessed | tf_op | source)
XLA Modules:
  0.0 118.5 jit_solution(3455670276979395588)
XLA Ops:
  0.6 0.0 copy-start.1
  0.6 0.0 copy-start
  1.4 0.7 fusion.5
  2.1 1.8 %pad_maximum_fusion.w_ref = bf16[96,2432]{1,0:T(8,128)(2,1)} fusion(bf16[96,128]{1,0:T(8,128)(2,1)S(1)} %fusion.5, bf16[96,768]{1,0:T(8,128)(2,1)} %bitcast.18, bf16[96,1536]{1,0:T(8,128)(2,1)} %param.9), kind=kLoop, calls=%fused_computation | loop fusion | flops 1400832 | bytes 933888 | tf_op jit(solution)/shard_map/concatenate | solution.py:576
  4.0 26.8 %gather_weights.1.w_ref = bf16[768,2432]{1,0:T(8,128)(2,1)} custom-call(bf16[96,2432]{1,0:T(8,128)(2,1)} %pad_maximum_fusion.w_ref), custom_call_target="tpu_custom_call" | custom-call | tf_op jit(solution)/shard_map/gather_weights/pallas_call | solution.py:122
  30.7 0.9 slice.24
  31.8 0.1 slice.27.taps_ref
  31.9 0.1 slice.29.gain_ref
  31.9 0.0 copy-done.1
  31.9 0.0 copy-done
  31.9 82.2 %layer.1 = (bf16[512,768]{1,0:T(8,128)(2,1)S(1)}, bf16[512,768]{1,0:T(8,128)(2,1)S(1)}, f32[96,1536]{1,0:T(8,128)S(1)}, f32[96,768]{1,0:T(8,128)S(1)}, f32[48,128]{1,0:T(8,128)S(1)}) custom-call(s32[1]{0:T(128)S(6)} %copy.20.len_ref, bf16[512,768]{1,0:T(8,128)(2,1)S(1)} %bitcast.14, bf16[512,768]{1,0:T(8,128)(2,1)S(1)} %bitcast.15, ...), custom_call_target="tpu_custom_call" | custom-call | tf_op jit(solution)/shard_map/layer/pallas_call | solution.py:520
  114.1 0.5 slice_bitcast_fusion
  114.6 0.6 slice.31
  115.2 0.9 copy.21
  116.1 0.9 copy.22
  117.0 0.8 copy.23
  117.8 0.7 copy.24
  (4 shorter events, 0.0 us)
Async XLA Ops:
  0.6 31.3 %copy-start.1 = (bf16[1,512,768]{2,1,0:T(8,128)(2,1)S(1)}, bf16[1,512,768]{2,1,0:T(8,128)(2,1)}, u32[]{:S(2)}) copy-start(bf16[1,512,768]{2,1,0:T(8,128)(2,1)} %param.13) | copy-start | bytes 2359300
  0.6 31.3 %copy-start = (bf16[1,512,768]{2,1,0:T(8,128)(2,1)S(1)}, bf16[1,512,768]{2,1,0:T(8,128)(2,1)}, u32[]{:S(2)}) copy-start(bf16[1,512,768]{2,1,0:T(8,128)(2,1)} %param.7) | copy-start | bytes 2359300

commit v4 on v3

--- a/solution.py
+++ b/solution.py
@@ -8,8 +8,8 @@
 from jax.sharding import PartitionSpec as P
 
 EPS = 1e-05
-WIDE = 2432
-CUT = 1280
+WIDE = 896
+CUT = 512
 MESH = pl.DeviceIdType.MESH
 
 
@@ -31,7 +31,7 @@
     pl.semaphore_wait(barrier, len(partners))
 
 
-def gather_kernel(w_ref, out_ref, local_sem, send_sem, recv_sem):
+def gather_steps(own_ref, first, out_ref, width, cut, local_sem, send_sem, recv_sem, base):
     x, y, z, core = place()
     y_lo = y % 2
     xp, xm, x2 = (x + 1) % 4, (x + 3) % 4, (x + 2) % 4
@@ -39,83 +39,95 @@
     to_xp, to_xm = device(xp, y, z, core), device(xm, y, z, core)
     to_yp, to_ym = device(x, yp, z, core), device(x, ym, z, core)
     to_sib = device(x, y, z, 1 - core)
-    greet([to_xp, to_xm, to_yp, to_ym, to_sib])
-
-    def rows(bx, byl):
-        return pl.ds(pl.multiple_of((bx * 2 + byl) * 96 + core * 48, 16), 48)
-
-    LO, HI, ALL = pl.ds(0, CUT), pl.ds(CUT, WIDE - CUT), pl.ds(0, WIDE)
-    own = pl.multiple_of((x * 2 + y_lo) * 96, 16)
-    local = pltpu.make_async_copy(w_ref, out_ref.at[pl.ds(own, 96)], local_sem)
-    local.start()
+    oth = 1 - y_lo
+    LO, HI, ALL = (0, cut), (cut, width - cut), (0, width)
     mine = pl.ds(pl.multiple_of(core * 48, 16), 48)
+    local = pltpu.make_async_copy(
+        own_ref.at[:, pl.ds(first, width)],
+        out_ref.at[pl.ds(pl.multiple_of((x * 2 + y_lo) * 96, 16), 96)], local_sem)
     sent = []
 
-    def send(index, bx, byl, cols, target, own_block=False):
-        dst = out_ref.at[rows(bx, byl), cols]
-        src = w_ref.at[mine, cols] if own_block else dst
-        copy = pltpu.make_async_remote_copy(
-            src_ref=src, dst_ref=dst, send_sem=send_sem.at[index], recv_sem=recv_sem.at[index],
+    def block(bx, byl, cols, who):
+        return out_ref.at[pl.ds(pl.multiple_of((bx * 2 + byl) * 96 + who * 48, 16), 48), pl.ds(*cols)]
+
+    def copy(index, src, dst, target):
+        return pltpu.make_async_remote_copy(
+            src_ref=src, dst_ref=dst, send_sem=send_sem.at[base + index], recv_sem=recv_sem.at[base + index],
             device_id=target, device_id_type=MESH)
-        copy.start()
-        sent.append(copy)
-
-    def arrive(index, bx, byl, cols):
-        dst = out_ref.at[rows(bx, byl), cols]
-        pltpu.make_async_remote_copy(
-            src_ref=dst, dst_ref=dst, send_sem=send_sem.at[index], recv_sem=recv_sem.at[index],
-            device_id=to_sib, device_id_type=MESH).wait_recv()
-
-    oth = 1 - y_lo
-    send(0, x, y_lo, ALL, to_xp, True)
-    send(1, x, y_lo, ALL, to_xm, True)
-    send(4, x, y_lo, LO, to_yp, True)
-    send(8, x, y_lo, HI, to_ym, True)
-    arrive(0, xm, y_lo, ALL)
-    send(2, xm, y_lo, LO, to_xp)
-    send(5, xm, y_lo, LO, to_yp)
-    send(9, xm, y_lo, HI, to_ym)
-    arrive(1, xp, y_lo, ALL)
-    send(3, xp, y_lo, HI, to_xm)
-    send(6, xp, y_lo, LO, to_yp)
-    send(10, xp, y_lo, HI, to_ym)
-    send(12, xm, y_lo, ALL, to_sib)
-    send(13, xp, y_lo, ALL, to_sib)
-    arrive(4, x, oth, LO)
-    send(16, x, oth, LO, to_sib)
-    arrive(8, x, oth, HI)
-    send(20, x, oth, HI, to_sib)
-    arrive(2, x2, y_lo, LO)
-    send(7, x2, y_lo, LO, to_yp)
-    send(14, x2, y_lo, LO, to_sib)
-    arrive(3, x2, y_lo, HI)
-    send(11, x2, y_lo, HI, to_ym)
-    send(15, x2, y_lo, HI, to_sib)
-    for k, bx in ((1, xm), (2, xp), (3, x2)):
-        arrive(4 + k, bx, oth, LO)
+
+    def send(index, bx, byl, cols, target, own=False):
+        dst = block(bx, byl, cols, core)
+        src = own_ref.at[mine, pl.ds(first + cols[0], cols[1])] if own else dst
+        c = copy(index, src, dst, target)
+        c.start()
+        sent.append(c)
+
+    def arrive(index, bx, byl, cols, who):
+        dst = block(bx, byl, cols, who)
+        copy(index, dst, dst, to_sib).wait_recv()
+
+    def begin():
+        local.start()
+        send(0, x, y_lo, ALL, to_xp, True)
+        send(1, x, y_lo, ALL, to_xm, True)
+        send(4, x, y_lo, LO, to_yp, True)
+        send(8, x, y_lo, HI, to_ym, True)
+
+    def across(k, bx):
+        arrive(4 + k, bx, oth, LO, core)
         send(16 + k, bx, oth, LO, to_sib)
-        arrive(8 + k, bx, oth, HI)
+        arrive(8 + k, bx, oth, HI, core)
         send(20 + k, bx, oth, HI, to_sib)
 
-    def sib_rows(bx, byl):
-        return pl.ds(pl.multiple_of((bx * 2 + byl) * 96 + (1 - core) * 48, 16), 48)
-
-    def arrive_sib(index, bx, byl, cols):
-        dst = out_ref.at[sib_rows(bx, byl), cols]
-        pltpu.make_async_remote_copy(
-            src_ref=dst, dst_ref=dst, send_sem=send_sem.at[index], recv_sem=recv_sem.at[index],
-            device_id=to_sib, device_id_type=MESH).wait_recv()
-
-    arrive_sib(12, xm, y_lo, ALL)
-    arrive_sib(13, xp, y_lo, ALL)
-    arrive_sib(14, x2, y_lo, LO)
-    arrive_sib(15, x2, y_lo, HI)
-    for k, bx in ((0, x), (1, xm), (2, xp), (3, x2)):
-        arrive_sib(16 + k, bx, oth, LO)
-        arrive_sib(20 + k, bx, oth, HI)
-    for copy in sent:
-        copy.wait_send()
-    local.wait()
+    def second():
+        arrive(0, xm, y_lo, ALL, core)
+        send(2, xm, y_lo, LO, to_xp)
+        send(5, xm, y_lo, LO, to_yp)
+        send(9, xm, y_lo, HI, to_ym)
+        arrive(1, xp, y_lo, ALL, core)
+        send(3, xp, y_lo, HI, to_xm)
+        send(6, xp, y_lo, LO, to_yp)
+        send(10, xp, y_lo, HI, to_ym)
+        send(12, xm, y_lo, ALL, to_sib)
+        send(13, xp, y_lo, ALL, to_sib)
+        across(0, x)
+
+    def third():
+        arrive(2, x2, y_lo, LO, core)
+        send(7, x2, y_lo, LO, to_yp)
+        send(14, x2, y_lo, LO, to_sib)
+        arrive(3, x2, y_lo, HI, core)
+        send(11, x2, y_lo, HI, to_ym)
+        send(15, x2, y_lo, HI, to_sib)
+        across(1, xm)
+        across(2, xp)
+
+    def fourth():
+        across(3, x2)
+
+    def last():
+        sib = 1 - core
+        arrive(12, xm, y_lo, ALL, sib)
+        arrive(13, xp, y_lo, ALL, sib)
+        arrive(14, x2, y_lo, LO, sib)
+        arrive(15, x2, y_lo, HI, sib)
+        for k, bx in ((0, x), (1, xm), (2, xp), (3, x2)):
+            arrive(16 + k, bx, oth, LO, sib)
+            arrive(20 + k, bx, oth, HI, sib)
+        local.wait()
+
+    return (begin, second, third, fourth, last), sent
+
+
+def gather_kernel(w_ref, out_ref, local_sem, send_sem, recv_sem):
+    x, y, z, core = place()
+    greet([device((x + 1) % 4, y, z, core), device((x + 3) % 4, y, z, core),
+           device(x, (y + 1) % 4, z, core), device(x, (y + 3) % 4, z, core), device(x, y, z, 1 - core)])
+    steps, sent = gather_steps(w_ref, 0, out_ref, WIDE, CUT, local_sem, send_sem, recv_sem, 0)
+    for step in steps:
+        step()
+    for c in sent:
+        c.wait_send()
 
 
 def gather_weights(packed):
@@ -149,12 +161,12 @@
 ROWS, START = (288, 288, 320), (0, 288, 576)
 
 
-def layer_kernel(factor, len_ref, x_ref, ct_ref, w_ref, taps_ref, gain_ref,
+def layer_kernel(factor, len_ref, x_ref, ct_ref, w_ref, own_ref, taps_ref, gain_ref,
                  res_ref, gin_ref, up_ref, down_ref, rest_ref,
                  normed, invs, scaled, scaled_t, cot_t, vals, gsig, dact, gat, dfl, act, dpv, dpg,
                  mixed, dsc, kacc, kall,
                  g, cr, cs, xr, xq, xs, yr, yq, zs, zr, fin,
-                 send_sem, recv_sem, zsend, zrecv, asend, arecv):
+                 send_sem, recv_sem, zsend, zrecv, asend, arecv, wq, wlocal, wsend, wrecv):
     f32, bf = jnp.float32, jnp.bfloat16
     length = len_ref[0]
     x, y, z, core = place()
@@ -285,17 +297,30 @@
                         row : row + 16, h * 128 : h * 128 + 128]
 
     R = 64
+    later = []
+    for q in range(2):
+        steps, copies = gather_steps(own_ref, q * 768, wq.at[q], 768, 384, wlocal.at[q], wsend, wrecv, q * 24)
+        later.append(steps)
+        sent.append(copies)
+    pl.semaphore_wait(barrier, 21)
+    later[0][0]()
     for b in range(3):
-        v_cols, g_cols, d_cols = pl.ds(b * 256, 256), pl.ds(768 + b * 256, 256), pl.ds(1536 + b * 256, 256)
+        if b:
+            later[b - 1][4]()
+
+        def weight(k):
+            cols = pl.ds(k * 256, 256)
+            return wq[b - 1, :, cols] if b else w_ref[:, cols]
+
         def gate(c, carry):
             base = pl.multiple_of(c * 128, 128)
             at = pl.ds(base, 128)
             live = live_of(base, 128)
-            v = dot(scaled[at, :], w_ref[:, v_cols], NN)
-            sg = jax.nn.sigmoid(dot(scaled[at, :], w_ref[:, g_cols], NN))
+            v = dot(scaled[at, :], weight(0), NN)
+            sg = jax.nn.sigmoid(dot(scaled[at, :], weight(1), NN))
             vals[at, :] = v
             gsig[at, :] = sg
-            dact[at, :] = dot(ct_ref[at, :], w_ref[:, d_cols], NN)
+            dact[at, :] = dot(ct_ref[at, :], weight(2), NN)
             for h in range(2):
                 cols = slice(h * 128, h * 128 + 128)
                 gat[h, pl.ds(base + 16, 128), :] = (v[:, cols] * sg[:, cols] * live).astype(bf).astype(f32)
@@ -330,6 +355,10 @@
                 return carry
 
             lax.fori_loop(0, 512 // R, forward, 0)
+            if b < 2:
+                later[b][1 + h]()
+            if b == 0 and h:
+                later[1][0]()
             kall[b * 2 + h] = jnp.sum(kacc[...], axis=1)
 
             def backward(c, carry):
@@ -360,12 +389,11 @@
         pack(b, dot(scaled_t[...], dpv[...], NN).astype(bf), 0)
         pack(b, dot(scaled_t[...], dpg[...], NN).astype(bf), 1)
         pack(b, dot(cot_t[...], act[...], NN).astype(bf), 2)
-        if b == 0:
-            pl.semaphore_wait(barrier, 21)
         if b < 2:
             core_start(b)
-        m = dot(act[...], w_ref[:, d_cols], NT)
-        d = dot(dpv[...], w_ref[:, v_cols], NT) + dot(dpg[...], w_ref[:, g_cols], NT)
+            later[b][3]()
+        m = dot(act[...], weight(2), NT)
+        d = dot(dpv[...], weight(0), NT) + dot(dpg[...], weight(1), NT)
         if b:
             mixed[...] += m
             dsc[...] += d
@@ -511,10 +539,11 @@
     for k in range(3):
         rest_ref[pl.ds(k * 16, 16), :] = tile(2, 36 + k)
     for c in sent:
-        c.wait_send()
-
-
-def layer(lengths, frames, cot, full, taps, gain, factor):
+        for one in c if isinstance(c, list) else [c]:
+            one.wait_send()
+
+
+def layer(lengths, frames, cot, full, own, taps, gain, factor):
     f32, bf = jnp.float32, jnp.bfloat16
     vmem = pl.BlockSpec(memory_space=pltpu.VMEM)
     return pl.pallas_call(
@@ -526,7 +555,7 @@
             jax.ShapeDtypeStruct((96, 768), f32),
             jax.ShapeDtypeStruct((48, 128), f32),
         ),
-        in_specs=[pl.BlockSpec(memory_space=pltpu.SMEM)] + [vmem] * 5,
+        in_specs=[pl.BlockSpec(memory_space=pltpu.SMEM)] + [vmem] * 6,
         out_specs=(vmem,) * 5,
         scratch_shapes=[
             pltpu.VMEM((512, 768), f32),
@@ -563,23 +592,29 @@
             pltpu.SemaphoreType.DMA((16,)),
             pltpu.SemaphoreType.DMA((16,)),
             pltpu.SemaphoreType.DMA((16,)),
+            pltpu.VMEM((2, 768, 768), bf),
+            pltpu.SemaphoreType.DMA((2,)),
+            pltpu.SemaphoreType.DMA((48,)),
+            pltpu.SemaphoreType.DMA((48,)),
         ],
         compiler_params=pltpu.CompilerParams(
             collective_id=1, has_side_effects=True, vmem_limit_bytes=48 * 1024 * 1024),
         name="layer",
-    )(lengths, frames, cot, full, taps, gain)
+    )(lengths, frames, cot, full, own, taps, gain)
 
 
 def body(frames_in, lengths, up_weight, norm_gain, conv_kernel, down_weight, cotangent):
     bf = jnp.bfloat16
     small = jnp.pad(jnp.concatenate([conv_kernel, norm_gain[None, :]], axis=0), ((0, 63), (0, 32)))
-    packed = jnp.concatenate([up_weight, down_weight.T, small], axis=1)
-    full = gather_weights(packed)
-    small = full[:, 2304:].reshape(8, 96, 128)[:, :33, :96].transpose(1, 0, 2).reshape(33, 768)
+    down = down_weight.T
+    parts = [a[:, at * 256 : at * 256 + 256] for b in range(3) for a, at in ((up_weight, b), (up_weight, 3 + b), (down, b))]
+    full = gather_weights(jnp.concatenate(parts[:3] + [small], axis=1))
+    own = jnp.concatenate(parts[3:], axis=1)
+    small = full[:, 768:].reshape(8, 96, 128)[:, :33, :96].transpose(1, 0, 2).reshape(33, 768)
     small = small.astype(jnp.float32)
     factor = 1.0 / 262144.0 ** 0.5
     result, grad_in, up_total, down_total, rest = layer(
-        lengths, frames_in.reshape(512, 768), cotangent.reshape(512, 768), full, small[:32], small[32:], factor
+        lengths, frames_in.reshape(512, 768), cotangent.reshape(512, 768), full, own, small[:32], small[32:], factor
     )
     return (
         result.reshape(1, 512, 768),

time: 119 us -> 128 us (1.076)
  local copies, waits for them, and re-layouts: 5.55 us -> 11.8 us
  Pallas kernels: 109 us -> 112 us
    pallas_call x1, Pallas kernels: 82.2 us -> 90.9 us  [layer(): pl.pallas_call(functools.partial(layer_kernel, factor), out_shape=(jax.Sh...]
    unnamed x8 -> x15, local copies, waits for them, and re-layouts: 3.29 us -> 8.69 us
    pallas_call x1, Pallas kernels: 26.8 us -> 21.5 us  [gather_weights(): pl.pallas_call(gather_kernel, out_shape=jax.ShapeDtypeStruct((768, WIDE),...]
where the time goes in v4:
time: 128 us; the launch traced here: 127 us
  Pallas kernels  112 us (88%)
  local copies, waits for them, and re-layouts  11.8 us (9%)
  other arithmetic  1.42 us (1%)
  between operations  1.36 us (1%)
    pallas_call x1, Pallas kernels, layer(): pl.pallas_call(functools.partial(layer_kernel, factor), out_shape=(jax.Sh...  90.9 us
    pallas_call x1, Pallas kernels, gather_weights(): pl.pallas_call(gather_kernel, out_shape=jax.ShapeDtypeStruct((768, WIDE),...  21.5 us
    unnamed x15, local copies, waits for them, and re-layouts  8.69 us

profile of v4, /device:TPU:1, one launch (start us, length us, event | category | flops | bytes accessed | tf_op | source)
XLA Modules:
  0.0 126.9 jit_solution(13806379741120477440)
XLA Ops:
  1.3 0.7 fusion.5
  2.0 0.8 slice_dynamic-update-slice_fusion.5
  2.8 0.8 slice_dynamic-update-slice_fusion.4
  3.6 0.8 slice_dynamic-update-slice_fusion.1
  4.4 0.8 slice_dynamic-update-slice_fusion.3
  5.2 0.9 slice_dynamic-update-slice_fusion.2
  6.1 0.8 slice_dynamic-update-slice_fusion
  6.9 0.7 pad_maximum_fusion.w_ref
  7.6 0.0 copy-start.1
  7.6 21.5 %gather_weights.1.w_ref = bf16[768,896]{1,0:T(8,128)(2,1)} custom-call(bf16[96,896]{1,0:T(8,128)(2,1)} %pad_maximum_fusion.w_ref), custom_call_target="tpu_custom_call" | custom-call | tf_op jit(solution)/shard_map/gather_weights/pallas_call | solution.py:134
  29.1 0.9 slice.60
  30.1 0.1 slice.63.taps_ref
  30.2 0.1 slice.65.gain_ref
  30.3 0.0 copy-done.1
  30.3 0.0 copy-done.2
  30.3 0.0 copy-start
  30.3 1.3 %copy-done = bf16[768,896]{1,0:T(8,128)(2,1)S(1)} copy-done((bf16[768,896]{1,0:T(8,128)(2,1)S(1)}, bf16[768,896]{1,0:T(8,128)(2,1)}, u32[]{:S(2)}) %copy-start) | copy-done | bytes 1376280
  31.6 90.9 %layer.1 = (bf16[512,768]{1,0:T(8,128)(2,1)S(1)}, bf16[512,768]{1,0:T(8,128)(2,1)S(1)}, f32[96,1536]{1,0:T(8,128)S(1)}, f32[96,768]{1,0:T(8,128)S(1)}, f32[48,128]{1,0:T(8,128)S(1)}) custom-call(s32[1]{0:T(128)S(6)} %copy.25.len_ref, bf16[512,768]{1,0:T(8,128)(2,1)S(1)} %bitcast.14, bf16[512,768]{1,0:T(8,128)(2,1)S(1)} %bitcast.15, ...), custom_call_target="tpu_custom_call" | custom-call | tf_op jit(solution)/shard_map/layer/pallas_call | solution.py:549
  122.5 0.5 slice_bitcast_fusion
  123.0 0.6 slice.67
  123.6 0.9 copy.26
  124.5 0.9 copy.27
  125.4 0.8 copy.28
  126.2 0.7 copy.29
  (5 shorter events, 0.0 us)
Async XLA Ops:
  7.6 22.7 %copy-start.1 = (bf16[1,512,768]{2,1,0:T(8,128)(2,1)S(1)}, bf16[1,512,768]{2,1,0:T(8,128)(2,1)}, u32[]{:S(2)}) copy-start(bf16[1,512,768]{2,1,0:T(8,128)(2,1)} %param.7) | copy-start | bytes 2359300
  7.6 22.7 %copy-start.2 = (bf16[1,512,768]{2,1,0:T(8,128)(2,1)S(1)}, bf16[1,512,768]{2,1,0:T(8,128)(2,1)}, u32[]{:S(2)}) copy-start(bf16[1,512,768]{2,1,0:T(8,128)(2,1)} %param.13) | copy-start | bytes 2359300
  30.3 1.3 %copy-start = (bf16[768,896]{1,0:T(8,128)(2,1)S(1)}, bf16[768,896]{1,0:T(8,128)(2,1)}, u32[]{:S(2)}) copy-start(bf16[768,896]{1,0:T(8,128)(2,1)} %gather_weights.1.w_ref) | copy-start | bytes 4128772

commit v5 on v3

--- a/solution.py
+++ b/solution.py
@@ -146,7 +146,7 @@
     lax.fori_loop(0, rows // step, one, 0)
 
 
-ROWS, START = (288, 288, 320), (0, 288, 576)
+ROWS, START, QUARTER = (288, 288, 320), (0, 288, 576), (144, 80)
 
 
 def layer_kernel(factor, len_ref, x_ref, ct_ref, w_ref, taps_ref, gain_ref,
@@ -225,14 +225,18 @@
 
     order = (x2, xp, xm, x)
 
-    def core_start(b):
-        n = pl.ds(0, ROWS[b])
+    def core_start(b, base, first, count):
+        n = pl.ds(first, count)
         for k, bx in enumerate(order):
-            send(b * 10 + k, g.at[b, bx, :, 1 - core, n], cr.at[b, bx, :, n], to_sib)
+            send(base + k, g.at[b, bx, :, 1 - core, n], cr.at[b, bx, :, n], to_sib)
 
     def core_sum(b, k):
         bx, n = order[k], ROWS[b]
-        arrive(b * 10 + k, cr.at[b, bx, :, pl.ds(0, n)])
+        if b == 2:
+            arrive(20 + k, cr.at[b, bx, :, pl.ds(0, 256)])
+            arrive(39 + k, cr.at[b, bx, :, pl.ds(256, 64)])
+        else:
+            arrive(b * 10 + k, cr.at[b, bx, :, pl.ds(0, n)])
         for j in range(2):
             def put(at, v):
                 cs[b, bx, j, at, :] = v.astype(bf)
@@ -362,8 +366,7 @@
         pack(b, dot(cot_t[...], act[...], NN).astype(bf), 2)
         if b == 0:
             pl.semaphore_wait(barrier, 21)
-        if b < 2:
-            core_start(b)
+        core_start(b, b * 10, 0, 256 if b == 2 else ROWS[b])
         m = dot(act[...], w_ref[:, d_cols], NT)
         d = dot(dpv[...], w_ref[:, v_cols], NT) + dot(dpg[...], w_ref[:, g_cols], NT)
         if b:
@@ -390,47 +393,64 @@
     small = jnp.concatenate([small, jnp.broadcast_to(gsum, (16, 768))], axis=0)
     for s in range(8):
         g[2, s // 2, s % 2, 1, pl.ds(256, 48), pl.ds(0, 96)] = small[:, s * 96 : s * 96 + 96].astype(bf)
-    core_start(2)
+    core_start(2, 39, 256, 64)
+
+    def y_part(p, yy, half):
+        q = QUARTER[p]
+        return xs.at[yy % 2, pl.ds(pl.multiple_of(p * 576 + (yy // 2) * (2 * q) + half * q, 16), q)]
+
+    def y_first(p):
+        n, r = 30 + p * 13, pl.ds(p * 144, QUARTER[p])
+        send(n, y_part(p, y2, 0), yq.at[0, r], to_yp)
+        send(n + 1, y_part(p, y2, 1), yq.at[1, r], to_ym)
+        send(n + 2, y_part(p, yp, 1), yr.at[0, 1, r], to_yp)
+        send(n + 3, y_part(p, ym, 0), yr.at[1, 0, r], to_ym)
+
+    def shifted(at, by, step):
+        return pl.ds(pl.multiple_of(at.start + by, 16), step)
+
+    def y_second(p):
+        n, r = 30 + p * 13, pl.ds(p * 144, QUARTER[p])
+        step = (48, 80)[p]
+        for k, yy, target in ((0, yp, to_yp), (1, ym, to_ym)):
+            arrive(n + k, yq.at[k, r])
+            dst = y_part(p, yy, k)
+
+            def put(at, v):
+                dst[at, :] = v.astype(bf)
+
+            add_rows(QUARTER[p], step, put,
+                     [lambda at: dst[at, :], lambda at: yq[k, shifted(at, p * 144, step), :]])
+            send(n + 4 + k, dst, yr.at[k, k, r], target)
+
+    def y_last(p):
+        n, r = 30 + p * 13, pl.ds(p * 144, QUARTER[p])
+        step = (48, 80)[p]
+        arrive(n + 2, yr.at[0, 1, r])
+        arrive(n + 3, yr.at[1, 0, r])
+        arrive(n + 4, yr.at[0, 0, r])
+        arrive(n + 5, yr.at[1, 1, r])
+        for half in range(2):
+            mine = y_part(p, y, half)
+
+            def put(at, v):
+                zs[shifted(at, p * 288 + half * QUARTER[p], step), :] = v.astype(bf)
+
+            add_rows(QUARTER[p], step, put,
+                     [lambda at: mine[at, :], lambda at: yr[0, half, shifted(at, p * 144, step), :],
+                      lambda at: yr[1, half, shifted(at, p * 144, step), :]])
+
     x_last(1)
+    y_first(0)
     x_first(2)
+    y_second(0)
     x_second(2)
+    y_last(0)
     x_last(2)
-    def part(yy, half, rows=224):
-        return xs.at[yy % 2, pl.ds(pl.multiple_of((yy // 2) * 448 + half * 224, 16), rows)]
-
-    send(30, part(y2, 0), yq.at[0], to_yp)
-    send(31, part(y2, 1), yq.at[1], to_ym)
-    send(32, part(yp, 1), yr.at[0, 1], to_yp)
-    send(33, part(ym, 0), yr.at[1, 0], to_ym)
-    arrive(30, yq.at[0])
-    dst_p = part(yp, 0)
-
-    def put_yp(at, v):
-        dst_p[at, :] = v.astype(jnp.bfloat16)
-
-    add_rows(224, 32, put_yp, [lambda at: dst_p[at, :], lambda at: yq[0, at, :]])
-    send(34, part(yp, 0), yr.at[0, 0], to_yp)
-    arrive(31, yq.at[1])
-    dst_m = part(ym, 1)
-
-    def put_ym(at, v):
-        dst_m[at, :] = v.astype(jnp.bfloat16)
-
-    add_rows(224, 32, put_ym, [lambda at: dst_m[at, :], lambda at: yq[1, at, :]])
-    send(35, part(ym, 1), yr.at[1, 1], to_ym)
-    arrive(32, yr.at[0, 1])
-    arrive(33, yr.at[1, 0])
-    arrive(34, yr.at[0, 0])
-    arrive(35, yr.at[1, 1])
-    zs[pl.ds(448, 64), :] = jnp.zeros((64, 128), jnp.bfloat16)
-    for half in range(2):
-        mine = part(y, half)
-
-        def put(at, v):
-            zs[pl.ds(pl.multiple_of(half * 224 + at.start, 16), 32), :] = v.astype(jnp.bfloat16)
-
-        add_rows(224, 32, put, [lambda at: mine[at, :], lambda at: yr[0, half, at, :], lambda at: yr[1, half, at, :]])
-
+    y_first(1)
+    zs[pl.ds(448, 64), :] = jnp.zeros((64, 128), bf)
+    y_second(1)
+    y_last(1)
 
     def piece(p):
         return pl.ds(pl.multiple_of(p * 32, 32), 32)
@@ -498,7 +518,11 @@
     def tile(b, t):
         per = ROWS[b] // 16
         row = START[b] + t % per * 16
-        return fin[t // per, row // 448, pl.ds(row % 448, 16), :].astype(f32) * factor
+        if row < 576:
+            half, row = row // 288, row % 288
+        else:
+            half, row = (row - 576) // 160, 288 + (row - 576) % 160
+        return fin[t // per, half, pl.ds(row, 16), :].astype(f32) * factor
 
     for b in range(3):
         for h in range(2):
@@ -557,8 +581,8 @@
             pltpu.VMEM((512, 128), bf),
             pltpu.VMEM((16, 32, 128), bf),
             pltpu.VMEM((2, 2, 512, 128), bf),
-            pltpu.SemaphoreType.DMA((39,)),
-            pltpu.SemaphoreType.DMA((39,)),
+            pltpu.SemaphoreType.DMA((49,)),
+            pltpu.SemaphoreType.DMA((49,)),
             pltpu.SemaphoreType.DMA((16,)),
             pltpu.SemaphoreType.DMA((16,)),
             pltpu.SemaphoreType.DMA((16,)),

time: 119 us -> 119 us (level)
  no operation moved by 1% of the time
where the time goes in v5:
time: 119 us
  Pallas kernels  109 us (92%)
  local copies, waits for them, and re-layouts  5.55 us (5%)
  other arithmetic  2.58 us (2%)
  between operations  1.47 us (1%)
    pallas_call x1, Pallas kernels, layer(): pl.pallas_call(functools.partial(layer_kernel, factor), out_shape=(jax.Sh...  82.2 us
    pallas_call x1, Pallas kernels, gather_weights(): pl.pallas_call(gather_kernel, out_shape=jax.ShapeDtypeStruct((768, WIDE),...  26.8 us
    unnamed x8, local copies, waits for them, and re-layouts  3.29 us

profile of v5, /device:TPU:1, one launch (start us, length us, event | category | flops | bytes accessed | tf_op | source)
XLA Modules:
  0.0 118.5 jit_solution(7623907797433422979)
XLA Ops:
  0.6 0.0 copy-start.1
  0.6 0.0 copy-start
  1.4 0.7 fusion.5
  2.1 1.8 %pad_maximum_fusion.w_ref = bf16[96,2432]{1,0:T(8,128)(2,1)} fusion(bf16[96,128]{1,0:T(8,128)(2,1)S(1)} %fusion.5, bf16[96,768]{1,0:T(8,128)(2,1)} %bitcast.18, bf16[96,1536]{1,0:T(8,128)(2,1)} %param.9), kind=kLoop, calls=%fused_computation | loop fusion | flops 1400832 | bytes 933888 | tf_op jit(solution)/shard_map/concatenate | solution.py:600
  4.0 26.8 %gather_weights.1.w_ref = bf16[768,2432]{1,0:T(8,128)(2,1)} custom-call(bf16[96,2432]{1,0:T(8,128)(2,1)} %pad_maximum_fusion.w_ref), custom_call_target="tpu_custom_call" | custom-call | tf_op jit(solution)/shard_map/gather_weights/pallas_call | solution.py:122
  30.7 0.9 slice.24
  31.8 0.1 slice.27.taps_ref
  31.9 0.1 slice.29.gain_ref
  31.9 0.0 copy-done.1
  31.9 0.0 copy-done
  31.9 82.2 %layer.1 = (bf16[512,768]{1,0:T(8,128)(2,1)S(1)}, bf16[512,768]{1,0:T(8,128)(2,1)S(1)}, f32[96,1536]{1,0:T(8,128)S(1)}, f32[96,768]{1,0:T(8,128)S(1)}, f32[48,128]{1,0:T(8,128)S(1)}) custom-call(s32[1]{0:T(128)S(6)} %copy.20.len_ref, bf16[512,768]{1,0:T(8,128)(2,1)S(1)} %bitcast.14, bf16[512,768]{1,0:T(8,128)(2,1)S(1)} %bitcast.15, ...), custom_call_target="tpu_custom_call" | custom-call | tf_op jit(solution)/shard_map/layer/pallas_call | solution.py:544
  114.1 0.5 slice_bitcast_fusion
  114.6 0.6 slice.31
  115.3 0.9 copy.21
  116.1 0.9 copy.22
  117.0 0.8 copy.23
  117.8 0.7 copy.24
  (4 shorter events, 0.0 us)
Async XLA Ops:
  0.6 31.3 %copy-start.1 = (bf16[1,512,768]{2,1,0:T(8,128)(2,1)S(1)}, bf16[1,512,768]{2,1,0:T(8,128)(2,1)}, u32[]{:S(2)}) copy-start(bf16[1,512,768]{2,1,0:T(8,128)(2,1)} %param.13) | copy-start | bytes 2359300
  0.6 31.3 %copy-start = (bf16[1,512,768]{2,1,0:T(8,128)(2,1)S(1)}, bf16[1,512,768]{2,1,0:T(8,128)(2,1)}, u32[]{:S(2)}) copy-start(bf16[1,512,768]{2,1,0:T(8,128)(2,1)} %param.7) | copy-start | bytes 2359300
